TPU v7x, 32 devices: a whole 2x2x4 slice. The times are simulated.
32 devices in a mesh: brow: 4 (over y, x), bcol: 8 (over z, core).
Axes of the slice: x: 2, y: 2, z: 4, core: 2. Of those that a mesh axis runs over, the one named last changes fastest.
Arguments:
- gradient: bfloat16 [2048, 2048], P(('brow', 'bcol')), may hold values from -1.5 to 1.5
- left_stats: float32 [4, 2048, 512], P('brow', 'bcol'), may hold values from -1 to 8, as said below
- right_stats: float32 [4, 2048, 512], P('brow', 'bcol'), may hold values from -1 to 8, as said below
- left_roots: bfloat16 [4, 2048, 512], P('brow', 'bcol'), may hold values from -1 to 3, as said below
- right_roots: bfloat16 [4, 2048, 512], P('brow', 'bcol'), may hold values from -1 to 3, as said below
- refresh: int32 [4, 1], P('brow'), may hold values from 0 to 3, as said below
Outputs:
- update: bfloat16 [2048, 2048], P(('brow', 'bcol'))
- new_left_stats: float32 [4, 2048, 512], P('brow', 'bcol')
- new_right_stats: float32 [4, 2048, 512], P('brow', 'bcol')
- new_left_roots: bfloat16 [4, 2048, 512], P('brow', 'bcol')
- new_right_roots: bfloat16 [4, 2048, 512], P('brow', 'bcol')
Inputs may be any that keep to these rules, and one draw needn't show every extreme that they name: `refresh`: each row names 1 different block columns; some block row lists column 3 and another block row lists column 0. `left_stats`: every 512 x 512 block is symmetric positive definite. `right_stats`: every 512 x 512 block is symmetric positive definite. `left_roots`: every 512 x 512 block is symmetric. `right_roots`: every 512 x 512 block is symmetric.
All inputs are finite; a program needn't handle non-finite values.
Results may differ from a plain program's by a relative error of at most 0.005.
Values may be sent and summed in bfloat16 or wider, within the bound.
No kernel may reach another device: no remote copies, remote signals or barrier semaphores. Data moves between devices by JAX's collectives and lax.ppermute only.
A program may use at most 64 MiB of HBM per device.

v0:
```python
import jax
import jax.numpy as jnp
from jax import lax
from jax.sharding import PartitionSpec as P

ITERS = 3


decay = 0.9
epsilon = 1e-06
highest = lax.Precision.HIGHEST


def from_partner(shard, axis, stride):
    return lax.ppermute(shard, axis, [(i, i ^ 1 << stride) for i in range(lax.axis_size(axis))])


def product(left_side, right_side):
    return jnp.dot(left_side, right_side, precision=highest)


def unchanged(matrix):
    return matrix


def inverse_rows(row_block, collect):
    row_count, order_size = row_block.shape
    eye_rows = (
        lax.broadcasted_iota(jnp.int32, (row_count, order_size), 0)
        == lax.broadcasted_iota(jnp.int32, (row_count, order_size), 1)
    ).astype(jnp.float32)
    eye_full = jnp.eye(order_size, dtype=jnp.float32)
    shifted = row_block + epsilon * eye_rows
    whole_matrix = collect(shifted)
    scaling = 2.5 / jnp.sqrt(jnp.sum(whole_matrix * whole_matrix))
    moment_full = scaling * whole_matrix
    iterate = jnp.sqrt(jnp.sqrt(scaling)) * eye_rows
    for iteration in range(ITERS):
        factor = (5.0 * eye_full - moment_full) * 0.25
        square = product(factor, factor)
        fourth_rows = product(square, square)
        moment_rows = product(fourth_rows, moment_full)
        iterate = product(iterate, factor)
        if iteration + 1 < ITERS:
            moment_full = collect(moment_rows)
    return iterate.astype(jnp.bfloat16)


def body(gradient, left_stats, right_stats, left_roots, right_roots, refresh):
    position = lax.axis_index("bcol")
    half = position % 2
    block_col = position // 2
    order_size = left_stats.shape[2]
    half_rows = order_size // 2
    is_second = half == 1
    mine = lax.all_to_all(gradient, "bcol", split_axis=1, concat_axis=0, tiled=True)
    left_root_mine = left_roots[0]
    partner_grad, partner_left = from_partner((mine, left_root_mine), "bcol", 0)
    grad_full = jnp.where(
        is_second,
        jnp.concatenate([partner_grad, mine], 1),
        jnp.concatenate([mine, partner_grad], 1),
    )
    left_root_full = jnp.where(
        is_second,
        jnp.concatenate([partner_left, left_root_mine], 0),
        jnp.concatenate([left_root_mine, partner_left], 0),
    )
    grad_rows = lax.dynamic_slice_in_dim(grad_full, half * half_rows, half_rows, 0)
    left_gram = lax.dot_general(
        grad_rows, grad_full, (((1,), (1,)), ((), ())), preferred_element_type=jnp.float32
    )
    right_gram = lax.dot_general(
        mine, grad_full, (((0,), (0,)), ((), ())), preferred_element_type=jnp.float32
    )
    left_new = decay * left_stats[0] + (1.0 - decay) * left_gram
    right_new = decay * right_stats[0] + (1.0 - decay) * right_gram
    right_part = lax.dot_general(
        grad_full, right_roots[0], (((1,), (1,)), ((), ())), preferred_element_type=jnp.float32
    ).astype(jnp.bfloat16)
    update_cols = jnp.dot(left_root_full, right_part, preferred_element_type=jnp.float32).astype(
        jnp.bfloat16
    )
    update = lax.all_to_all(update_cols, "bcol", split_axis=0, concat_axis=1, tiled=True)
    chosen = refresh[0]
    listed = jnp.any(chosen == block_col)
    mine_side = jnp.where(is_second, right_new, left_new)
    partner_side = from_partner(
        jnp.where(is_second, left_new, right_new).astype(jnp.bfloat16), "bcol", 0
    ).astype(jnp.float32)
    whole_side = jnp.where(
        is_second,
        jnp.concatenate([partner_side, mine_side], 0),
        jnp.concatenate([mine_side, partner_side], 0),
    )
    root_full = inverse_rows(whole_side, unchanged)
    own_rows = lax.dynamic_slice_in_dim(root_full, half * half_rows, half_rows, 0)
    given_rows = lax.dynamic_slice_in_dim(root_full, (1 - half) * half_rows, half_rows, 0)
    taken = from_partner(given_rows, "bcol", 0)
    left_fresh = jnp.where(is_second, taken, own_rows)
    right_fresh = jnp.where(is_second, own_rows, taken)
    left_out = jnp.where(listed, left_fresh, left_roots[0])
    right_out = jnp.where(listed, right_fresh, right_roots[0])
    return (update, left_new[None], right_new[None], left_out[None], right_out[None])


def solution(mesh):
    in_specs = (
        P(("brow", "bcol"), None),
        P("brow", "bcol", None),
        P("brow", "bcol", None),
        P("brow", "bcol", None),
        P("brow", "bcol", None),
        P("brow", None),
    )
    out_specs = (
        P(("brow", "bcol"), None),
        P("brow", "bcol", None),
        P("brow", "bcol", None),
        P("brow", "bcol", None),
        P("brow", "bcol", None),
    )
    return jax.shard_map(body, mesh=mesh, in_specs=in_specs, out_specs=out_specs, check_vma=False)
```

profile of v0, /device:TPU:0, one launch (start us, length us, event | category | flops | bytes accessed | tf_op | source)
XLA Modules:
  0.0 51.4 jit_solution(1072921021482301779)
XLA Ops:
  0.6 1.7 %copy.16 = bf16[8,8,8,256]{3,2,0,1:T(8,128)(2,1)} copy(bf16[8,8,8,256]{3,2,1,0:T(8,128)(2,1)} %bitcast.59) | data formatting | bytes 524288 | tf_op jit(solution)/shard_map/all_to_all | solution.py:56
  2.3 6.5 %all-to-all-start = ((bf16[64,8,256]{2,0,1:T(8,128)(2,1)}), bf16[64,8,256]{2,0,1:T(8,128)(2,1)S(1)}, u32[]{:S(2)}, u32[]{:S(2)}) async-start(bf16[64,8,256]{2,0,1:T(8,128)(2,1)} %bitcast.48), calls=%async_computation | async-start | bytes 524288 | tf_op jit(solution)/shard_map/all_to_all | solution.py:56
  8.8 0.5 collective-permute-start
  9.3 9.2 %all-to-all-done = bf16[64,8,256]{2,0,1:T(8,128)(2,1)S(1)} async-done(((bf16[64,8,256]{2,0,1:T(8,128)(2,1)}), bf16[64,8,256]{2,0,1:T(8,128)(2,1)S(1)}, u32[]{:S(2)}, u32[]{:S(2)}) %all-to-all-start) | async-done | bytes 262176 | tf_op jit(solution)/shard_map/all_to_all | solution.py:56
  18.5 1.5 %collective-permute-done.1 = bf16[512,256]{1,0:T(8,128)(2,1)S(1)} collective-permute-done((bf16[512,256]{1,0:T(8,128)(2,1)S(1)}, bf16[512,256]{1,0:T(8,128)(2,1)S(1)}, u32[]{:S(2)}, u32[]{:S(2)}) %collective-permute-start.1) | collective-permute-done | bytes 262176 | tf_op jit(solution)/shard_map/ppermute | solution.py:15
  20.0 1.5 %convolution_convert_fusion.1 = bf16[512,256]{1,0:T(8,128)(2,1)} fusion(bf16[256,512]{1,0:T(8,128)(2,1)S(1)} %bitcast.58, bf16[256,512]{1,0:T(8,128)(2,1)S(1)} %collective-permute-done, pred[]{:T(512)S(6)} %eq.23, bf16[1,256,512]{2,1,0:T(8,128)(2,1)S(1)} %copy-done.5, bf16[512,256]{1,0:T(8,128)(2,1)S(1)} %bitcast.54, ...), kind=kOutput, calls=%fused_computation.10 | convolution fusion | flops 273416192 | bytes 1572865 | tf_op jit(solution)/shard_map/dot_general | solution.py:81
  21.5 3.4 %all-to-all-start.1 = ((bf16[8,64,256]{2,1,0:T(8,128)(2,1)}), bf16[8,64,256]{2,1,0:T(8,128)(2,1)S(1)}, u32[]{:S(2)}, u32[]{:S(2)}) async-start(bf16[8,64,256]{2,1,0:T(8,128)(2,1)} %bitcast.5), calls=%async_computation.1 | async-start | bytes 524288 | tf_op jit(solution)/shard_map/all_to_all | solution.py:84
  25.0 0.1 maximum_select_fusion.3
  25.1 0.9 %copy-done.7 = f32[1,256,512]{2,1,0:T(8,128)S(1)} copy-done((f32[1,256,512]{2,1,0:T(8,128)S(1)}, f32[1,256,512]{2,1,0:T(8,128)}, u32[]{:S(2)}) %copy-start.7) | copy-done | bytes 524312
  26.0 0.3 fusion.2
  26.3 0.7 %copy-done.2 = f32[1,256,512]{2,1,0:T(8,128)S(1)} copy-done((f32[1,256,512]{2,1,0:T(8,128)S(1)}, f32[1,256,512]{2,1,0:T(8,128)}, u32[]{:S(2)}) %copy-start.2) | copy-done | bytes 524312
  27.0 0.4 select_convert_fusion
  27.4 0.0 copy-start.1
  27.4 0.5 collective-permute-start.2
  27.9 0.1 broadcast_select_fusion
  28.0 0.2 copy-done.1
  28.2 0.8 %collective-permute-done.2 = bf16[256,512]{1,0:T(8,128)(2,1)S(1)} collective-permute-done((bf16[256,512]{1,0:T(8,128)(2,1)S(1)}, bf16[256,512]{1,0:T(8,128)(2,1)S(1)}, u32[]{:S(2)}, u32[]{:S(2)}) %collective-permute-start.2) | collective-permute-done | bytes 262176 | tf_op jit(solution)/shard_map/ppermute | solution.py:15
  29.1 0.9 %multiply_reduce_fusion = f32[]{:T(128)} fusion(f32[256,512]{1,0:T(8,128)S(1)} %convert_element_type.20, f32[256,512]{1,0:T(8,128)S(1)} %broadcast_select_fusion, pred[]{:T(512)S(6)} %eq.23), kind=kLoop, calls=%fused_computation.18 | loop fusion | flops 2097151 | bytes 1048581 | tf_op jit(solution)/shard_map/reduce_sum | solution.py:35
  30.7 2.1 %fusion.15 = f32[512,512]{1,0:T(8,128)S(1)} fusion(f32[]{:T(128)S(6)} %div.14, f32[256,512]{1,0:T(8,128)S(1)} %broadcast_select_fusion, f32[256,512]{1,0:T(8,128)S(1)} %convert_element_type.20, pred[]{:T(512)S(6)} %eq.23), kind=kOutput, calls=%fused_computation.24 | convolution fusion | flops 1613234176 | bytes 2097157 | tf_op jit(solution)/shard_map/dot_general | solution.py:19
  32.8 1.9 %fusion.7 = f32[512,512]{1,0:T(8,128)S(1)} fusion(f32[]{:T(128)S(6)} %div.14, f32[]{:T(128)S(6)} %sqrt.11, f32[256,512]{1,0:T(8,128)S(1)} %broadcast_select_fusion, f32[256,512]{1,0:T(8,128)S(1)} %convert_element_type.20, pred[]{:T(512)S(6)} %eq.23), kind=kOutput, calls=%fused_computation.16 | convolution fusion | flops 1613758464 | bytes 2097161 | tf_op jit(solution)/shard_map/dot_general | solution.py:19
  34.8 1.8 %fusion.61 = f32[512,512]{1,0:T(8,128)S(1)} fusion(f32[512,512]{1,0:T(8,128)S(1)} %fusion.15), kind=kOutput, calls=%fused_computation.72 | convolution fusion | flops 1610612736 | bytes 2097152 | tf_op jit(solution)/shard_map/dot_general | solution.py:19
  36.6 1.9 %fusion.9 = f32[512,512]{1,0:T(8,128)S(1)} fusion(f32[512,512]{1,0:T(8,128)S(1)} %fusion.61, f32[]{:T(128)S(6)} %div.14, f32[256,512]{1,0:T(8,128)S(1)} %broadcast_select_fusion, f32[256,512]{1,0:T(8,128)S(1)} %convert_element_type.20, pred[]{:T(512)S(6)} %eq.23), kind=kOutput, calls=%fused_computation.20 | convolution fusion | flops 1612447744 | bytes 3145733 | tf_op jit(solution)/shard_map/dot_general | solution.py:19
  38.6 1.9 %fusion.11 = f32[512,512]{1,0:T(8,128)S(1)} fusion(f32[512,512]{1,0:T(8,128)S(1)} %fusion.9), kind=kOutput, calls=%fused_computation.22 | convolution fusion | flops 1611661312 | bytes 2097152 | tf_op jit(solution)/shard_map/dot_general | solution.py:19
  40.5 1.9 %fusion.13 = f32[512,512]{1,0:T(8,128)S(1)} fusion(f32[512,512]{1,0:T(8,128)S(1)} %fusion.7, f32[512,512]{1,0:T(8,128)S(1)} %fusion.9), kind=kOutput, calls=%fused_computation.23 | convolution fusion | flops 1611661312 | bytes 3145728 | tf_op jit(solution)/shard_map/dot_general | solution.py:19
  42.4 2.0 %fusion.62 = f32[512,512]{1,0:T(8,128)S(1)} fusion(f32[512,512]{1,0:T(8,128)S(1)} %fusion.11), kind=kOutput, calls=%fused_computation.73 | convolution fusion | flops 1610612736 | bytes 2097152 | tf_op jit(solution)/shard_map/dot_general | solution.py:19
  44.5 1.9 %fusion = f32[512,512]{1,0:T(8,128)S(1)} fusion(f32[512,512]{1,0:T(8,128)S(1)} %fusion.62, f32[512,512]{1,0:T(8,128)S(1)} %fusion.9), kind=kOutput, calls=%fused_computation.3 | convolution fusion | flops 1611661312 | bytes 3145728 | tf_op jit(solution)/shard_map/dot_general | solution.py:19
  46.3 1.9 %convolution_convert_fusion = bf16[512,512]{1,0:T(8,128)(2,1)S(1)} fusion(f32[512,512]{1,0:T(8,128)S(1)} %fusion.13, f32[512,512]{1,0:T(8,128)S(1)} %fusion), kind=kOutput, calls=%fused_computation.4 | convolution fusion | flops 1610874880 | bytes 2621440 | tf_op jit(solution)/shard_map/dot_general | solution.py:19
  48.2 0.4 collective-permute-start.3
  49.4 0.7 %copy.14 = bf16[8,8,8,256]{3,2,0,1:T(8,128)(2,1)} copy(bf16[8,8,8,256]{3,2,1,0:T(8,128)(2,1)S(1)} %bitcast.52) | data formatting | bytes 524288 | tf_op jit(solution)/shard_map/all_to_all | solution.py:84
  50.1 0.3 copy-done.4
  50.4 0.1 copy-done.6
  50.5 0.9 %fusion.42 = (bf16[1,256,512]{2,1,0:T(8,128)(2,1)}, bf16[1,256,512]{2,1,0:T(8,128)(2,1)}) fusion(bf16[1,256,512]{2,1,0:T(8,128)(2,1)S(1)} %copy-done.6, bf16[256,512]{1,0:T(8,128)(2,1)S(1)} %collective-permute-done.3, pred[]{:T(512)S(6)} %eq.23, pred[]{:T(512)} %bitcast.14, bf16[512,512]{1,0:T(8,128)(2,1)S(1)} %convolution_convert_fusion, s32[]{:T(128)S(6)} %select_n.72, ...), kind=kLoop, calls=%fused_computation.53 | loop fusion | flops 524288 | bytes 1572870 | tf_op jit(solution)/shard_map/broadcast_in_dim | solution.py:104
  (16 shorter events, 0.1 us)
Async XLA Ops:
  2.3 6.5 %copy-start.3 = (bf16[1,256,512]{2,1,0:T(8,128)(2,1)S(1)}, bf16[1,256,512]{2,1,0:T(8,128)(2,1)}, u32[]{:S(2)}) copy-start(bf16[1,256,512]{2,1,0:T(8,128)(2,1)} %param.9) | copy-start | bytes 786436
  2.3 17.7 %copy-start.5 = (bf16[1,256,512]{2,1,0:T(8,128)(2,1)S(1)}, bf16[1,256,512]{2,1,0:T(8,128)(2,1)}, u32[]{:S(2)}) copy-start(bf16[1,256,512]{2,1,0:T(8,128)(2,1)} %param.10) | copy-start | bytes 786436
  2.3 16.2 %all-to-all-start = ((bf16[64,8,256]{2,0,1:T(8,128)(2,1)}), bf16[64,8,256]{2,0,1:T(8,128)(2,1)S(1)}, u32[]{:S(2)}, u32[]{:S(2)}) async-start(bf16[64,8,256]{2,0,1:T(8,128)(2,1)} %bitcast.48), calls=%async_computation | async-start | bytes 524288 | tf_op jit(solution)/shard_map/all_to_all | solution.py:56
  8.8 9.7 %collective-permute-start = (bf16[256,512]{1,0:T(8,128)(2,1)S(1)}, bf16[256,512]{1,0:T(8,128)(2,1)S(1)}, u32[]{:S(2)}, u32[]{:S(2)}) collective-permute-start(bf16[256,512]{1,0:T(8,128)(2,1)S(1)} %bitcast.57), channel_id=1, source_target_pairs={{0,1},{1,0},{2,3},{3,2},{4,5},{5,4},{6,7},{7,6},{8,9},{9,8},{10,11... | collective-permute-start | bytes 786440 | tf_op jit(solution)/shard_map/ppermute | solution.py:15
  18.5 1.5 %collective-permute-start.1 = (bf16[512,256]{1,0:T(8,128)(2,1)S(1)}, bf16[512,256]{1,0:T(8,128)(2,1)S(1)}, u32[]{:S(2)}, u32[]{:S(2)}) collective-permute-start(bf16[512,256]{1,0:T(8,128)(2,1)S(1)} %bitcast.53), channel_id=1, source_target_pairs={{0,1},{1,0},{2,3},{3,2},{4,5},{5,4},{6,7},{7,6},{8,9},{9,8},{10,11... | collective-permute-start | bytes 786440 | tf_op jit(solution)/shard_map/ppermute | solution.py:15
  21.5 27.8 %all-to-all-start.1 = ((bf16[8,64,256]{2,1,0:T(8,128)(2,1)}), bf16[8,64,256]{2,1,0:T(8,128)(2,1)S(1)}, u32[]{:S(2)}, u32[]{:S(2)}) async-start(bf16[8,64,256]{2,1,0:T(8,128)(2,1)} %bitcast.5), calls=%async_computation.1 | async-start | bytes 524288 | tf_op jit(solution)/shard_map/all_to_all | solution.py:84
  24.9 1.0 %copy-start.7 = (f32[1,256,512]{2,1,0:T(8,128)S(1)}, f32[1,256,512]{2,1,0:T(8,128)}, u32[]{:S(2)}) copy-start(f32[1,256,512]{2,1,0:T(8,128)} %param.8) | copy-start | bytes 1572868
  26.0 1.0 %copy-start.2 = (f32[1,256,512]{2,1,0:T(8,128)S(1)}, f32[1,256,512]{2,1,0:T(8,128)}, u32[]{:S(2)}) copy-start(f32[1,256,512]{2,1,0:T(8,128)} %param.7) | copy-start | bytes 1572868
  27.0 0.8 %copy-start = (f32[256,512]{1,0:T(8,128)}, f32[256,512]{1,0:T(8,128)S(1)}, u32[]{:S(2)}) copy-start(f32[256,512]{1,0:T(8,128)S(1)} %fusion.2) | copy-start | bytes 1572868
  27.4 0.8 %copy-start.1 = (f32[256,512]{1,0:T(8,128)}, f32[256,512]{1,0:T(8,128)S(1)}, u32[]{:S(2)}) copy-start(f32[256,512]{1,0:T(8,128)S(1)} %get-tuple-element.8) | copy-start | bytes 1572868
  27.4 1.6 %collective-permute-start.2 = (bf16[256,512]{1,0:T(8,128)(2,1)S(1)}, bf16[256,512]{1,0:T(8,128)(2,1)S(1)}, u32[]{:S(2)}, u32[]{:S(2)}) collective-permute-start(bf16[256,512]{1,0:T(8,128)(2,1)S(1)} %get-tuple-element.7), channel_id=1, source_target_pairs={{0,1},{1,0},{2,3},{3,2},{4,5},{5,4},{6,7},{7,6},{8,9},{9,8},{10,11... | collective-permute-start | bytes 786440 | tf_op jit(solution)/shard_map/ppermute | solution.py:15
  48.2 1.9 %collective-permute-start.3 = (bf16[256,512]{1,0:T(8,128)(2,1)S(1)}, bf16[256,512]{1,0:T(8,128)(2,1)S(1)}, u32[]{:S(2)}, u32[]{:S(2)}) collective-permute-start(bf16[256,512]{1,0:T(8,128)(2,1)S(1)} %constant_dynamic-slice_fusion), channel_id=1, source_target_pairs={{0,1},{1,0},{2,3},{3,2},{4,5},{5,4},{6,7},{7,6},{8,9},{9,8},{10,11... | collective-permute-start | bytes 786440 | tf_op jit(solution)/shard_map/ppermute | solution.py:15
  49.4 1.0 %copy-start.4 = (bf16[1,256,512]{2,1,0:T(8,128)(2,1)S(1)}, bf16[1,256,512]{2,1,0:T(8,128)(2,1)}, u32[]{:S(2)}) copy-start(bf16[1,256,512]{2,1,0:T(8,128)(2,1)} %param.9) | copy-start | bytes 786436
  49.4 1.1 %copy-start.6 = (bf16[1,256,512]{2,1,0:T(8,128)(2,1)S(1)}, bf16[1,256,512]{2,1,0:T(8,128)(2,1)}, u32[]{:S(2)}) copy-start(bf16[1,256,512]{2,1,0:T(8,128)(2,1)} %param.10) | copy-start | bytes 786436
where the time goes:
time: 51.9 us; the launch traced here: 51.4 us
  matrix products  19.5 us (38%)
  waiting for transfers between devices  11.6 us (22%)
  starting transfers between devices  11.3 us (22%)
  local copies, waits for them, and re-layouts  4.65 us (9%)
  between operations  2.24 us (4%)
  other arithmetic  2.1 us (4%)
    dot_general x9, matrix products, product(): return jnp.dot(left_side, right_side, precision=highest)  17.4 us
    all_to_all x1, waiting for transfers between devices, body(): lax.all_to_all(gradient, 'bcol', split_axis=1, concat_axis=0, tiled=True)  9.2 us
    all_to_all x1, starting transfers between devices, body(): lax.all_to_all(gradient, 'bcol', split_axis=1, concat_axis=0, tiled=True)  6.49 us
    all_to_all x1, starting transfers between devices, body(): lax.all_to_all(update_cols, 'bcol', split_axis=0, concat_axis=1, tiled=True)  3.41 us
    ppermute x4, waiting for transfers between devices, from_partner(): lax.ppermute(shard, axis, [(i, i ^ 1 << stride) for i in range(lax.axis_s...  2.38 us
    unnamed x16, local copies, waits for them, and re-layouts  2.23 us
    all_to_all x1, local copies, waits for them, and re-layouts, body(): lax.all_to_all(gradient, 'bcol', split_axis=1, concat_axis=0, tiled=True)  1.67 us
    dot_general x1, matrix products, body(): jnp.dot(left_root_full, right_part, preferred_element_type=jnp.float32)  1.48 us
  transfers between devices with their start and end apart: 6, of which 3 were waited for; matrix products, arithmetic and copies ran while one was open for 39% of the time, Pallas kernels for 0%

commit v1 on v0

v1 whole, which is shorter than its diff:
```python
import jax
import jax.numpy as jnp
from jax import lax
from jax.experimental import pallas as pl
from jax.experimental.pallas import tpu as pltpu
from jax.sharding import PartitionSpec as P

ITERS = 3
decay = 0.9
epsilon = 1e-06
F32 = jnp.float32
BF16 = jnp.bfloat16
VMEM = pl.BlockSpec(memory_space=pltpu.VMEM)
SMEM = pl.BlockSpec(memory_space=pltpu.SMEM)


def place():
    position = lax.axis_index("bcol")
    return position >> 1, position & 1


def chip_pairs(step):
    return [(i, i ^ (step << 1)) for i in range(lax.axis_size("bcol"))]


def core_pairs():
    return [(i, i ^ 1) for i in range(lax.axis_size("bcol"))]


def dot(left_side, right_side, contract=((1,), (0,))):
    return lax.dot_general(left_side, right_side, (contract, ((), ())), preferred_element_type=F32)


def call(kernel, out_shape, scratch, cost, name):
    flops, moved = cost
    return lambda *operands: pl.pallas_call(
        kernel,
        out_shape=out_shape,
        in_specs=[SMEM if o.dtype == jnp.int32 else VMEM for o in operands],
        out_specs=jax.tree.map(lambda _: VMEM, out_shape),
        scratch_shapes=scratch,
        name=name,
        cost_estimate=pl.CostEstimate(flops=flops, bytes_accessed=moved, transcendentals=0),
    )(*operands)


def prepare(chips, rows, order, left_mine, left_other, right_mine, right_other, old_left, old_right, old_other,
            left_rows, right_full, side, left_full):
    column, half = place()
    span = order // 2
    mine = pl.ds(pl.multiple_of(half * span, span), span)
    other = pl.ds(pl.multiple_of((1 - half) * span, span), span)
    left_full[mine, :] = left_mine[...]
    left_full[other, :] = left_other[...]
    right_full[mine, :] = right_mine[...]
    right_full[other, :] = right_other[...]
    for step in range(chips):
        start = pl.multiple_of(((column ^ step) * 2 + half) * rows, rows)
        left_rows[step * rows : (step + 1) * rows, :] = left_full[pl.ds(start, rows), :]
    side[other, :] = old_other[...]


def precondition(chips, rows, order, *refs):
    mine, other = refs[:chips], refs[chips : 2 * chips]
    left_rows, right_full = refs[2 * chips : 2 * chips + 2]
    updates, whole = refs[2 * chips + 2 : 3 * chips + 2], refs[3 * chips + 2]
    column, half = place()
    for step in range(chips):
        start = (column ^ step) * 2
        whole[pl.ds(pl.multiple_of((start + half) * rows, rows), rows), :] = mine[step][...]
        whole[pl.ds(pl.multiple_of((start + 1 - half) * rows, rows), rows), :] = other[step][...]
    mixed = dot(whole[...], right_full[...]).astype(BF16)
    result = dot(left_rows[...], mixed).astype(BF16)
    for step in range(chips):
        updates[step][...] = result[step * rows : (step + 1) * rows, :]


def refreshed(order, whole, old_left, old_right, old_side, new_left, new_right, root_mine, root_other, stat, weight, root):
    column, half = place()
    span = order // 2
    mine = pl.ds(pl.multiple_of(half * span, span), span)
    other = pl.ds(pl.multiple_of((1 - half) * span, span), span)
    rate = 1.0 - decay
    full = whole[...]
    new_left[...] = decay * old_left[...] + rate * dot(whole[mine, :], full, ((1,), (1,)))
    new_right[...] = decay * old_right[...] + rate * dot(whole[:, mine], full, ((0,), (0,)))

    @pl.when(half == 0)
    def _():
        stat[mine, :] = new_left[...]
        stat[other, :] = decay * old_side[other, :] + rate * dot(whole[other, :], full, ((1,), (1,)))

    @pl.when(half == 1)
    def _():
        stat[mine, :] = new_right[...]
        stat[other, :] = decay * old_side[other, :] + rate * dot(whole[:, other], full, ((0,), (0,)))

    shape = (order, order)
    diagonal = lax.broadcasted_iota(jnp.int32, shape, 0) == lax.broadcasted_iota(jnp.int32, shape, 1)
    shifted = stat[...] + jnp.where(diagonal, epsilon, 0.0)
    total = jnp.sum(jnp.sum(shifted * shifted, axis=1, keepdims=True), axis=0, keepdims=True)
    scaling = 2.5 / jnp.sqrt(total)
    stat[...] = scaling * shifted
    held = 1.25
    weight[...] = -0.25 * stat[...]
    square = 25.0 / 16.0
    for iteration in range(1, ITERS):
        moment = stat[...]
        narrow = moment.astype(BF16)
        change = (dot(narrow, narrow) - 10.0 * moment) * (1.0 / 16.0)
        small = change.astype(BF16)
        fourth = (2.0 * square) * change + dot(small, small)
        moment = (square * square) * moment + dot(fourth.astype(BF16), narrow)
        stat[...] = moment
        product = dot(weight[...].astype(BF16), moment.astype(BF16))
        weight[...] = 1.25 * weight[...] - (0.25 * held) * moment - 0.25 * product
        held = 1.25 * held
    scale = jnp.sqrt(jnp.sqrt(scaling))
    root[...] = (scale * (weight[...] + jnp.where(diagonal, held, 0.0))).astype(BF16)
    root_mine[...] = root[mine, :]
    root_other[...] = root[other, :]


def body(gradient, left_stats, right_stats, left_roots, right_roots, refresh):
    column, half = place()
    chips = lax.axis_size("bcol") // 2
    rows = gradient.shape[0]
    order = left_stats.shape[2]
    span = order // 2
    is_second = half == 1
    left_old, right_old = left_stats[0], right_stats[0]
    left_root, right_root = left_roots[0], right_roots[0]

    def piece(step):
        return lax.dynamic_slice(gradient, (0, (column ^ step) * order), (rows, order))

    pieces = [piece(step) for step in range(chips)]
    mine = [pieces[0]] + [lax.ppermute(pieces[step], "bcol", chip_pairs(step)) for step in range(1, chips)]
    given_stat = jnp.where(is_second, left_old, right_old).astype(BF16)
    left_other, right_other, old_other = [
        lax.ppermute(x, "bcol", core_pairs()) for x in (left_root, right_root, given_stat)
    ]
    other = [lax.ppermute(x, "bcol", core_pairs()) for x in mine]

    def shape(r, c, t):
        return jax.ShapeDtypeStruct((r, c), t)

    def kernel(f, *static):
        return lambda *refs: f(*static, *refs)

    left_rows, right_full, old_side = call(
        kernel(prepare, chips, rows, order),
        (shape(span, order, BF16), shape(order, order, BF16), shape(order, order, F32)),
        [pltpu.VMEM((order, order), BF16)],
        (0, 4 * order * order * 2),
        "prepare",
    )(left_root, left_other, right_root, right_other, left_old, right_old, old_other.astype(F32))
    *updates, whole = call(
        kernel(precondition, chips, rows, order),
        (*[shape(rows, order, BF16)] * chips, shape(order, order, BF16)),
        [],
        (3 * order**3, 4 * order * order * 2),
        "precondition",
    )(*mine, *other, left_rows, right_full)
    returned = [updates[0]] + [lax.ppermute(updates[step], "bcol", chip_pairs(step)) for step in range(1, chips)]
    left_new, right_new, root_mine, root_other = call(
        kernel(refreshed, order),
        (shape(span, order, F32), shape(span, order, F32), shape(span, order, BF16), shape(span, order, BF16)),
        [pltpu.VMEM((order, order), F32), pltpu.VMEM((order, order), F32), pltpu.VMEM((order, order), BF16)],
        (20 * order**3, 8 * order * order * 4),
        "refreshed",
    )(whole, left_old, right_old, old_side)
    taken = lax.ppermute(root_other, "bcol", core_pairs())
    listed = jnp.any(refresh[0] == column)
    left_out = jnp.where(listed, jnp.where(is_second, taken, root_mine), left_root)
    right_out = jnp.where(listed, jnp.where(is_second, root_mine, taken), right_root)
    update = jnp.zeros((rows, chips * order), BF16)
    for step in range(chips):
        update = lax.dynamic_update_slice(update, returned[step], (0, (column ^ step) * order))
    return (update, left_new[None], right_new[None], left_out[None], right_out[None])


def solution(mesh):
    block = P("brow", "bcol", None)
    rows = P(("brow", "bcol"), None)
    in_specs = (rows, block, block, block, block, P("brow", None))
    out_specs = (rows, block, block, block, block)
    return jax.shard_map(body, mesh=mesh, in_specs=in_specs, out_specs=out_specs, check_vma=False)
```

time: 51.9 us -> 43.7 us (0.84)
  matrix products: 19.5 us -> 0 us
  Pallas kernels: 0 us -> 12.4 us
  starting transfers between devices: 11.3 us -> 16.5 us
  waiting for transfers between devices: 11.6 us -> 8.38 us
  local copies, waits for them, and re-layouts: 4.65 us -> 1.48 us
  other arithmetic: 2.1 us -> 3.06 us
  between operations: 2.24 us -> 1.58 us
    dot_general x12 -> x0, matrix products: 19.5 us -> none  [the longest x9 17.4 us: product(): return jnp.dot(left_side, right_side, precision=highest)]
    ppermute x4 -> x14, starting transfers between devices: 1.42 us -> 16.5 us  [the longest x3 10.1 us: body(): lax.ppermute(pieces[step], 'bcol', chip_pairs(step))]
    pallas_call x0 -> x3, Pallas kernels: none -> 12.4 us  [call(): pl.pallas_call(kernel, out_shape=out_shape, in_specs=[SMEM if o.dtype ==...]
    all_to_all x2 -> x0, starting transfers between devices: 9.9 us -> none  [the longest x1 6.49 us: body(): lax.all_to_all(gradient, 'bcol', split_axis=1, concat_axis=0, tiled=True)]
    all_to_all x2 -> x0, waiting for transfers between devices: 9.2 us -> none  [the longest x1 9.2 us: body(): lax.all_to_all(gradient, 'bcol', split_axis=1, concat_axis=0, tiled=True)]
    ppermute x4 -> x14, waiting for transfers between devices: 2.38 us -> 8.38 us  [the longest x3 6.03 us: body(): lax.ppermute(updates[step], 'bcol', chip_pairs(step))]
    all_to_all x2 -> x0, local copies, waits for them, and re-layouts: 2.39 us -> none  [the longest x1 1.67 us: body(): lax.all_to_all(gradient, 'bcol', split_axis=1, concat_axis=0, tiled=True)]
    convert_element_type x1 -> x2, other arithmetic: 0.05 us -> 2.2 us  [the longest x1 1.34 us: body(): given_stat = jnp.where(is_second, left_old, right_old).astype(BF16)]
  transfers between devices with their start and end apart: 6 -> 14, of which waited for: 3 -> 4; matrix products, arithmetic and copies ran while one was open for 39% -> 2% of each run, Pallas kernels for 0% -> 7%
where the time goes in v1:
time: 43.7 us; the launch traced here: 43.4 us
  starting transfers between devices  16.5 us (38%)
  Pallas kernels  12.4 us (28%)
  waiting for transfers between devices  8.38 us (19%)
  other arithmetic  3.06 us (7%)
  between operations  1.58 us (4%)
  local copies, waits for them, and re-layouts  1.48 us (3%)
    pallas_call x3, Pallas kernels, call(): pl.pallas_call(kernel, out_shape=out_shape, in_specs=[SMEM if o.dtype ==...  12.4 us
    ppermute x3, starting transfers between devices, body(): lax.ppermute(pieces[step], 'bcol', chip_pairs(step))  10.1 us
    ppermute x3, waiting for transfers between devices, body(): lax.ppermute(updates[step], 'bcol', chip_pairs(step))  6.03 us
    ppermute x3, starting transfers between devices, body(): lax.ppermute(updates[step], 'bcol', chip_pairs(step))  4.38 us
    ppermute x3, waiting for transfers between devices, body(): lax.ppermute(pieces[step], 'bcol', chip_pairs(step))  2.33 us
    unnamed x42, local copies, waits for them, and re-layouts  1.4 us
    convert_element_type x1, other arithmetic, body(): given_stat = jnp.where(is_second, left_old, right_old).astype(BF16)  1.34 us
    ppermute x3, starting transfers between devices, body(): lax.ppermute(x, 'bcol', core_pairs())  1.07 us
  transfers between devices with their start and end apart: 14, of which 4 were waited for; matrix products, arithmetic and copies ran while one was open for 2% of the time, Pallas kernels for 7%

profile of v1, /device:TPU:0, one launch (start us, length us, event | category | flops | bytes accessed | tf_op | source)
XLA Modules:
  0.0 43.4 jit_solution(11480843409430970129)
XLA Ops:
  0.6 0.0 copy-start
  0.6 0.0 copy-start.2
  0.7 1.3 %select_convert_fusion = bf16[256,512]{1,0:T(8,128)(2,1)S(1)} fusion(pred[]{:T(512)S(6)} %eq.9, f32[1,256,512]{2,1,0:T(8,128)} %param.8, f32[1,256,512]{2,1,0:T(8,128)} %param.7), kind=kLoop, calls=%fused_computation | loop fusion | flops 131072 | bytes 1310721 | tf_op jit(solution)/shard_map/convert_element_type | solution.py:139
  2.0 0.6 %collective-permute-start.9 = (bf16[256,512]{1,0:T(8,128)(2,1)S(1)}, bf16[256,512]{1,0:T(8,128)(2,1)S(1)}, u32[]{:S(2)}, u32[]{:S(2)}) collective-permute-start(bf16[256,512]{1,0:T(8,128)(2,1)S(1)} %select_convert_fusion), channel_id=1, source_target_pairs={{0,1},{1,0},{2,3},{3,2},{4,5},{5,4},{6,7},{7,6},{8,9},{9,8},{10,11... | collective-permute-start | bytes 786440 | tf_op jit(solution)/shard_map/ppermute | solution.py:141
  2.6 0.1 collective-permute-start.7
  2.7 0.4 collective-permute-start.8
  3.1 2.7 %collective-permute-start = (bf16[64,512]{1,0:T(8,128)(2,1)S(1)}, bf16[64,512]{1,0:T(8,128)(2,1)S(1)}, u32[]{:S(2)}, u32[]{:S(2)}) collective-permute-start(bf16[64,512]{1,0:T(8,128)(2,1)S(1)} %get-tuple-element.32), channel_id=1, source_target_pairs={{0,2},{1,3},{2,0},{3,1},{4,6},{5,7},{6,4},{7,5},{8,10},{9,11},{10,... | collective-permute-start | bytes 196616 | tf_op jit(solution)/shard_map/ppermute | solution.py:138
  5.8 2.6 %collective-permute-start.1 = (bf16[64,512]{1,0:T(8,128)(2,1)S(1)}, bf16[64,512]{1,0:T(8,128)(2,1)S(1)}, u32[]{:S(2)}, u32[]{:S(2)}) collective-permute-start(bf16[64,512]{1,0:T(8,128)(2,1)S(1)} %get-tuple-element.34), channel_id=1, source_target_pairs={{0,4},{1,5},{2,6},{3,7},{4,0},{5,1},{6,2},{7,3},{8,12},{9,13},{10,... | collective-permute-start | bytes 196616 | tf_op jit(solution)/shard_map/ppermute | solution.py:138
  8.4 0.1 collective-permute-done.refs_1_
  8.5 4.8 %collective-permute-start.2 = (bf16[64,512]{1,0:T(8,128)(2,1)S(1)}, bf16[64,512]{1,0:T(8,128)(2,1)S(1)}, u32[]{:S(2)}, u32[]{:S(2)}) collective-permute-start(bf16[64,512]{1,0:T(8,128)(2,1)S(1)} %get-tuple-element.31), channel_id=1, source_target_pairs={{0,6},{1,7},{2,4},{3,5},{4,2},{5,3},{6,0},{7,1},{8,14},{9,15},{10,... | collective-permute-start | bytes 196616 | tf_op jit(solution)/shard_map/ppermute | solution.py:138
  13.3 2.2 %collective-permute-done.2.refs_3_ = bf16[64,512]{1,0:T(8,128)(2,1)S(1)} collective-permute-done((bf16[64,512]{1,0:T(8,128)(2,1)S(1)}, bf16[64,512]{1,0:T(8,128)(2,1)S(1)}, u32[]{:S(2)}, u32[]{:S(2)}) %collective-permute-start.2) | collective-permute-done | bytes 65568 | tf_op jit(solution)/shard_map/ppermute | solution.py:138
  15.5 0.5 %collective-permute-start.5 = (bf16[64,512]{1,0:T(8,128)(2,1)S(1)}, bf16[64,512]{1,0:T(8,128)(2,1)S(1)}, u32[]{:S(2)}, u32[]{:S(2)}) collective-permute-start(bf16[64,512]{1,0:T(8,128)(2,1)S(1)} %collective-permute-done.1.refs_2_), channel_id=1, source_target_pairs={{0,1},{1,0},{2,3},{3,2},{4,5},{5,4},{6,7},{7,6},{8,9},{9,8},{10,11... | collective-permute-start | bytes 196616 | tf_op jit(solution)/shard_map/ppermute | solution.py:143
  16.0 0.1 collective-permute-start.6
  16.8 0.9 %convert_element_type.7.refs_6_ = f32[256,512]{1,0:T(8,128)} convert(bf16[256,512]{1,0:T(8,128)(2,1)S(1)} %collective-permute-done.9) | non-fusion elementwise | flops 131072 | bytes 786432 | tf_op jit(solution)/shard_map/convert_element_type | solution.py:157
  17.7 0.0 copy-start.5
  17.7 0.7 %copy-done.5 = bf16[256,512]{1,0:T(8,128)(2,1)} copy-done((bf16[256,512]{1,0:T(8,128)(2,1)}, bf16[256,512]{1,0:T(8,128)(2,1)S(1)}, u32[]{:S(2)}) %copy-start.5) | copy-done | bytes 262168
  18.4 3.0 %prepare.1 = (bf16[256,512]{1,0:T(8,128)(2,1)}, bf16[512,512]{1,0:T(8,128)(2,1)}, f32[512,512]{1,0:T(8,128)}) custom-call(bf16[256,512]{1,0:T(8,128)(2,1)} %bitcast.22, bf16[256,512]{1,0:T(8,128)(2,1)} %copy-done.4, bf16[256,512]{1,0:T(8,128)(2,1)} %bitcast.24, bf16[256,512]{1,0:T(8,128)(2,1)} %copy-done.5, f32[256,512]{1,0:T(8,128)} %bitcast.18, ...), custom_call_target="tpu_custom_call" | custom-call | bytes 2097152 | tf_op jit(solution)/shard_map/prepare/pallas_call | solution.py:36
  21.4 0.0 copy-start.18
  21.4 0.6 %copy-done.14 = bf16[64,512]{1,0:T(8,128)(2,1)} copy-done((bf16[64,512]{1,0:T(8,128)(2,1)}, bf16[64,512]{1,0:T(8,128)(2,1)S(1)}, u32[]{:S(2)}) %copy-start.14) | copy-done | bytes 65560
  22.0 0.0 copy-done.16
  22.0 0.0 copy-done.18
  22.0 0.0 copy-done.20
  22.0 2.9 %precondition.1 = (bf16[64,512]{1,0:T(8,128)(2,1)}, bf16[64,512]{1,0:T(8,128)(2,1)}, bf16[64,512]{1,0:T(8,128)(2,1)}, bf16[64,512]{1,0:T(8,128)(2,1)}, bf16[512,512]{1,0:T(8,128)(2,1)}) custom-call(bf16[64,512]{1,0:T(8,128)(2,1)} %copy-done.10, bf16[64,512]{1,0:T(8,128)(2,1)} %copy-done.11, bf16[64,512]{1,0:T(8,128)(2,1)} %copy-done.12, ...), custom_call_target="tpu_custom_call" | custom-call | flops 402653184 | bytes 2097152 | tf_op jit(solution)/shard_map/precondition/pallas_call | solution.py:36
  25.0 6.6 %refreshed.1 = (f32[256,512]{1,0:T(8,128)}, f32[256,512]{1,0:T(8,128)}, bf16[256,512]{1,0:T(8,128)(2,1)}, bf16[256,512]{1,0:T(8,128)(2,1)}) custom-call(bf16[512,512]{1,0:T(8,128)(2,1)} %get-tuple-element.23.refs_0_, f32[256,512]{1,0:T(8,128)} %bitcast.19, f32[256,512]{1,0:T(8,128)} %bitcast.21, f32[512,512]{1,0:T(8,128)} %get-tuple-element.24.refs_3_), custom_call_target="tpu_custom_call" | custom-call | flops 2684354560 | bytes 8388608 | tf_op jit(solution)/shard_map/refreshed/pallas_call | solution.py:36
  31.6 0.4 collective-permute-start.13
  32.0 4.4 %collective-permute-start.11 = (bf16[64,512]{1,0:T(8,128)(2,1)S(1)}, bf16[64,512]{1,0:T(8,128)(2,1)S(1)}, u32[]{:S(2)}, u32[]{:S(2)}) collective-permute-start(bf16[64,512]{1,0:T(8,128)(2,1)S(1)} %copy-done.17), channel_id=1, source_target_pairs={{0,4},{1,5},{2,6},{3,7},{4,0},{5,1},{6,2},{7,3},{8,12},{9,13},{10,... | collective-permute-start | bytes 196616 | tf_op jit(solution)/shard_map/ppermute | solution.py:165
  36.3 0.0 collective-permute-start.12
  36.4 0.0 copy-start.1
  36.5 3.9 %collective-permute-done.11 = bf16[64,512]{1,0:T(8,128)(2,1)S(1)} collective-permute-done((bf16[64,512]{1,0:T(8,128)(2,1)S(1)}, bf16[64,512]{1,0:T(8,128)(2,1)S(1)}, u32[]{:S(2)}, u32[]{:S(2)}) %collective-permute-start.11) | collective-permute-done | bytes 65568 | tf_op jit(solution)/shard_map/ppermute | solution.py:165
  40.4 2.1 %collective-permute-done.12 = bf16[64,512]{1,0:T(8,128)(2,1)S(1)} collective-permute-done((bf16[64,512]{1,0:T(8,128)(2,1)S(1)}, bf16[64,512]{1,0:T(8,128)(2,1)S(1)}, u32[]{:S(2)}, u32[]{:S(2)}) %collective-permute-start.12) | collective-permute-done | bytes 65568 | tf_op jit(solution)/shard_map/ppermute | solution.py:165
  42.5 0.0 copy-start.7
  42.6 0.9 %select_bitcast_fusion = (bf16[1,256,512]{2,1,0:T(8,128)(2,1)}, bf16[1,256,512]{2,1,0:T(8,128)(2,1)}) fusion(bf16[256,512]{1,0:T(8,128)(2,1)S(1)} %copy-done.8, bf16[256,512]{1,0:T(8,128)(2,1)S(1)} %collective-permute-done.13, pred[]{:T(512)} %bitcast.8, pred[]{:T(512)S(6)} %eq.9, bf16[1,256,512]{2,1,0:T(8,128)(2,1)S(1)} %copy-done.3, ...), kind=kLoop, calls=%fused_computation.1 | loop fusion | flops 524288 | bytes 1572866 | tf_op jit(solution)/shard_map/broadcast_in_dim | solution.py:180
  (50 shorter events, 0.2 us)
Async XLA Ops:
  0.6 1.9 %copy-start = (bf16[1,256,512]{2,1,0:T(8,128)(2,1)S(1)}, bf16[1,256,512]{2,1,0:T(8,128)(2,1)}, u32[]{:S(2)}) copy-start(bf16[1,256,512]{2,1,0:T(8,128)(2,1)} %param.9) | copy-start | bytes 786436
  0.6 2.0 %copy-start.2 = (bf16[1,256,512]{2,1,0:T(8,128)(2,1)S(1)}, bf16[1,256,512]{2,1,0:T(8,128)(2,1)}, u32[]{:S(2)}) copy-start(bf16[1,256,512]{2,1,0:T(8,128)(2,1)} %param.10) | copy-start | bytes 786436
  0.7 2.4 %copy-start.6 = (bf16[64,2048]{1,0:T(8,128)(2,1)S(1)}, bf16[64,2048]{1,0:T(8,128)(2,1)}, u32[]{:S(2)}) copy-start(bf16[64,2048]{1,0:T(8,128)(2,1)} %param.6) | copy-start | bytes 786436
  2.0 13.5 %collective-permute-start.9 = (bf16[256,512]{1,0:T(8,128)(2,1)S(1)}, bf16[256,512]{1,0:T(8,128)(2,1)S(1)}, u32[]{:S(2)}, u32[]{:S(2)}) collective-permute-start(bf16[256,512]{1,0:T(8,128)(2,1)S(1)} %select_convert_fusion), channel_id=1, source_target_pairs={{0,1},{1,0},{2,3},{3,2},{4,5},{5,4},{6,7},{7,6},{8,9},{9,8},{10,11... | collective-permute-start | bytes 786440 | tf_op jit(solution)/shard_map/ppermute | solution.py:141
  2.6 13.5 %collective-permute-start.7 = (bf16[256,512]{1,0:T(8,128)(2,1)S(1)}, bf16[256,512]{1,0:T(8,128)(2,1)S(1)}, u32[]{:S(2)}, u32[]{:S(2)}) collective-permute-start(bf16[256,512]{1,0:T(8,128)(2,1)S(1)} %bitcast.23), channel_id=1, source_target_pairs={{0,1},{1,0},{2,3},{3,2},{4,5},{5,4},{6,7},{7,6},{8,9},{9,8},{10,11... | collective-permute-start | bytes 786440 | tf_op jit(solution)/shard_map/ppermute | solution.py:141
  2.7 15.0 %collective-permute-start.8 = (bf16[256,512]{1,0:T(8,128)(2,1)S(1)}, bf16[256,512]{1,0:T(8,128)(2,1)S(1)}, u32[]{:S(2)}, u32[]{:S(2)}) collective-permute-start(bf16[256,512]{1,0:T(8,128)(2,1)S(1)} %bitcast.25), channel_id=1, source_target_pairs={{0,1},{1,0},{2,3},{3,2},{4,5},{5,4},{6,7},{7,6},{8,9},{9,8},{10,11... | collective-permute-start | bytes 786440 | tf_op jit(solution)/shard_map/ppermute | solution.py:141
  3.1 14.6 %copy-start.10 = (bf16[64,512]{1,0:T(8,128)(2,1)}, bf16[64,512]{1,0:T(8,128)(2,1)S(1)}, u32[]{:S(2)}) copy-start(bf16[64,512]{1,0:T(8,128)(2,1)S(1)} %get-tuple-element.33.refs_0_) | copy-start | bytes 196612
  3.1 5.4 %collective-permute-start = (bf16[64,512]{1,0:T(8,128)(2,1)S(1)}, bf16[64,512]{1,0:T(8,128)(2,1)S(1)}, u32[]{:S(2)}, u32[]{:S(2)}) collective-permute-start(bf16[64,512]{1,0:T(8,128)(2,1)S(1)} %get-tuple-element.32), channel_id=1, source_target_pairs={{0,2},{1,3},{2,0},{3,1},{4,6},{5,7},{6,4},{7,5},{8,10},{9,11},{10,... | collective-permute-start | bytes 196616 | tf_op jit(solution)/shard_map/ppermute | solution.py:138
  5.8 7.4 %collective-permute-start.1 = (bf16[64,512]{1,0:T(8,128)(2,1)S(1)}, bf16[64,512]{1,0:T(8,128)(2,1)S(1)}, u32[]{:S(2)}, u32[]{:S(2)}) collective-permute-start(bf16[64,512]{1,0:T(8,128)(2,1)S(1)} %get-tuple-element.34), channel_id=1, source_target_pairs={{0,4},{1,5},{2,6},{3,7},{4,0},{5,1},{6,2},{7,3},{8,12},{9,13},{10,... | collective-permute-start | bytes 196616 | tf_op jit(solution)/shard_map/ppermute | solution.py:138
  8.5 9.2 %copy-start.11 = (bf16[64,512]{1,0:T(8,128)(2,1)}, bf16[64,512]{1,0:T(8,128)(2,1)S(1)}, u32[]{:S(2)}) copy-start(bf16[64,512]{1,0:T(8,128)(2,1)S(1)} %collective-permute-done.refs_1_) | copy-start | bytes 196612
  8.5 7.0 %collective-permute-start.2 = (bf16[64,512]{1,0:T(8,128)(2,1)S(1)}, bf16[64,512]{1,0:T(8,128)(2,1)S(1)}, u32[]{:S(2)}, u32[]{:S(2)}) collective-permute-start(bf16[64,512]{1,0:T(8,128)(2,1)S(1)} %get-tuple-element.31), channel_id=1, source_target_pairs={{0,6},{1,7},{2,4},{3,5},{4,2},{5,3},{6,0},{7,1},{8,14},{9,15},{10,... | collective-permute-start | bytes 196616 | tf_op jit(solution)/shard_map/ppermute | solution.py:138
  13.3 4.4 %copy-start.12 = (bf16[64,512]{1,0:T(8,128)(2,1)}, bf16[64,512]{1,0:T(8,128)(2,1)S(1)}, u32[]{:S(2)}) copy-start(bf16[64,512]{1,0:T(8,128)(2,1)S(1)} %collective-permute-done.1.refs_2_) | copy-start | bytes 196612
  13.3 8.1 %collective-permute-start.3 = (bf16[64,512]{1,0:T(8,128)(2,1)S(1)}, bf16[64,512]{1,0:T(8,128)(2,1)S(1)}, u32[]{:S(2)}, u32[]{:S(2)}) collective-permute-start(bf16[64,512]{1,0:T(8,128)(2,1)S(1)} %get-tuple-element.33.refs_0_), channel_id=1, source_target_pairs={{0,1},{1,0},{2,3},{3,2},{4,5},{5,4},{6,7},{7,6},{8,9},{9,8},{10,11... | collective-permute-start | bytes 196616 | tf_op jit(solution)/shard_map/ppermute | solution.py:143
  15.5 2.2 %copy-start.13 = (bf16[64,512]{1,0:T(8,128)(2,1)}, bf16[64,512]{1,0:T(8,128)(2,1)S(1)}, u32[]{:S(2)}) copy-start(bf16[64,512]{1,0:T(8,128)(2,1)S(1)} %collective-permute-done.2.refs_3_) | copy-start | bytes 196612
  15.5 5.8 %collective-permute-start.4 = (bf16[64,512]{1,0:T(8,128)(2,1)S(1)}, bf16[64,512]{1,0:T(8,128)(2,1)S(1)}, u32[]{:S(2)}, u32[]{:S(2)}) collective-permute-start(bf16[64,512]{1,0:T(8,128)(2,1)S(1)} %collective-permute-done.refs_1_), channel_id=1, source_target_pairs={{0,1},{1,0},{2,3},{3,2},{4,5},{5,4},{6,7},{7,6},{8,9},{9,8},{10,11... | collective-permute-start | bytes 196616 | tf_op jit(solution)/shard_map/ppermute | solution.py:143
  15.5 5.9 %collective-permute-start.5 = (bf16[64,512]{1,0:T(8,128)(2,1)S(1)}, bf16[64,512]{1,0:T(8,128)(2,1)S(1)}, u32[]{:S(2)}, u32[]{:S(2)}) collective-permute-start(bf16[64,512]{1,0:T(8,128)(2,1)S(1)} %collective-permute-done.1.refs_2_), channel_id=1, source_target_pairs={{0,1},{1,0},{2,3},{3,2},{4,5},{5,4},{6,7},{7,6},{8,9},{9,8},{10,11... | collective-permute-start | bytes 196616 | tf_op jit(solution)/shard_map/ppermute | solution.py:143
  16.0 1.6 %copy-start.4 = (bf16[256,512]{1,0:T(8,128)(2,1)}, bf16[256,512]{1,0:T(8,128)(2,1)S(1)}, u32[]{:S(2)}) copy-start(bf16[256,512]{1,0:T(8,128)(2,1)S(1)} %collective-permute-done.7.refs_1_) | copy-start | bytes 786436
  16.0 5.4 %collective-permute-start.6 = (bf16[64,512]{1,0:T(8,128)(2,1)S(1)}, bf16[64,512]{1,0:T(8,128)(2,1)S(1)}, u32[]{:S(2)}, u32[]{:S(2)}) collective-permute-start(bf16[64,512]{1,0:T(8,128)(2,1)S(1)} %collective-permute-done.2.refs_3_), channel_id=1, source_target_pairs={{0,1},{1,0},{2,3},{3,2},{4,5},{5,4},{6,7},{7,6},{8,9},{9,8},{10,11... | collective-permute-start | bytes 196616 | tf_op jit(solution)/shard_map/ppermute | solution.py:143
  17.7 0.7 %copy-start.5 = (bf16[256,512]{1,0:T(8,128)(2,1)}, bf16[256,512]{1,0:T(8,128)(2,1)S(1)}, u32[]{:S(2)}) copy-start(bf16[256,512]{1,0:T(8,128)(2,1)S(1)} %collective-permute-done.8.refs_3_) | copy-start | bytes 786436
  21.4 0.6 %copy-start.16 = (bf16[64,512]{1,0:T(8,128)(2,1)}, bf16[64,512]{1,0:T(8,128)(2,1)S(1)}, u32[]{:S(2)}) copy-start(bf16[64,512]{1,0:T(8,128)(2,1)S(1)} %collective-permute-done.4.refs_5_) | copy-start | bytes 196612
  24.9 7.0 %copy-start.19 = (bf16[64,512]{1,0:T(8,128)(2,1)S(1)}, bf16[64,512]{1,0:T(8,128)(2,1)}, u32[]{:S(2)}) copy-start(bf16[64,512]{1,0:T(8,128)(2,1)} %get-tuple-element.20) | copy-start | bytes 196612
  24.9 7.0 %copy-start.17 = (bf16[64,512]{1,0:T(8,128)(2,1)S(1)}, bf16[64,512]{1,0:T(8,128)(2,1)}, u32[]{:S(2)}) copy-start(bf16[64,512]{1,0:T(8,128)(2,1)} %get-tuple-element.21) | copy-start | bytes 196612
  24.9 11.4 %copy-start.15 = (bf16[64,512]{1,0:T(8,128)(2,1)S(1)}, bf16[64,512]{1,0:T(8,128)(2,1)}, u32[]{:S(2)}) copy-start(bf16[64,512]{1,0:T(8,128)(2,1)} %get-tuple-element.22) | copy-start | bytes 196612
  25.0 11.4 %copy-start.9 = (bf16[64,512]{1,0:T(8,128)(2,1)S(1)}, bf16[64,512]{1,0:T(8,128)(2,1)}, u32[]{:S(2)}) copy-start(bf16[64,512]{1,0:T(8,128)(2,1)} %get-tuple-element.19) | copy-start | bytes 196612
  31.6 11.0 %collective-permute-start.13 = (bf16[256,512]{1,0:T(8,128)(2,1)}, bf16[256,512]{1,0:T(8,128)(2,1)S(1)}, u32[]{:S(2)}, u32[]{:S(2)}) collective-permute-start(bf16[256,512]{1,0:T(8,128)(2,1)} %get-tuple-element.27), channel_id=1, source_target_pairs={{0,1},{1,0},{2,3},{3,2},{4,5},{5,4},{6,7},{7,6},{8,9},{9,8},{10,11... | collective-permute-start | bytes 786440 | tf_op jit(solution)/shard_map/ppermute | solution.py:173
  32.0 4.5 %collective-permute-start.10 = (bf16[64,512]{1,0:T(8,128)(2,1)S(1)}, bf16[64,512]{1,0:T(8,128)(2,1)S(1)}, u32[]{:S(2)}, u32[]{:S(2)}) collective-permute-start(bf16[64,512]{1,0:T(8,128)(2,1)S(1)} %copy-done.19), channel_id=1, source_target_pairs={{0,2},{1,3},{2,0},{3,1},{4,6},{5,7},{6,4},{7,5},{8,10},{9,11},{10,... | collective-permute-start | bytes 196616 | tf_op jit(solution)/shard_map/ppermute | solution.py:165
  32.0 8.4 %collective-permute-start.11 = (bf16[64,512]{1,0:T(8,128)(2,1)S(1)}, bf16[64,512]{1,0:T(8,128)(2,1)S(1)}, u32[]{:S(2)}, u32[]{:S(2)}) collective-permute-start(bf16[64,512]{1,0:T(8,128)(2,1)S(1)} %copy-done.17), channel_id=1, source_target_pairs={{0,4},{1,5},{2,6},{3,7},{4,0},{5,1},{6,2},{7,3},{8,12},{9,13},{10,... | collective-permute-start | bytes 196616 | tf_op jit(solution)/shard_map/ppermute | solution.py:165
  36.3 6.2 %collective-permute-start.12 = (bf16[64,512]{1,0:T(8,128)(2,1)S(1)}, bf16[64,512]{1,0:T(8,128)(2,1)S(1)}, u32[]{:S(2)}, u32[]{:S(2)}) collective-permute-start(bf16[64,512]{1,0:T(8,128)(2,1)S(1)} %copy-done.15), channel_id=1, source_target_pairs={{0,6},{1,7},{2,4},{3,5},{4,2},{5,3},{6,0},{7,1},{8,14},{9,15},{10,... | collective-permute-start | bytes 196616 | tf_op jit(solution)/shard_map/ppermute | solution.py:165
  36.4 6.2 %copy-start.8 = (bf16[256,512]{1,0:T(8,128)(2,1)S(1)}, bf16[256,512]{1,0:T(8,128)(2,1)}, u32[]{:S(2)}) copy-start(bf16[256,512]{1,0:T(8,128)(2,1)} %get-tuple-element.28) | copy-start | bytes 786436
  36.4 6.2 %copy-start.1 = (bf16[1,256,512]{2,1,0:T(8,128)(2,1)S(1)}, bf16[1,256,512]{2,1,0:T(8,128)(2,1)}, u32[]{:S(2)}) copy-start(bf16[1,256,512]{2,1,0:T(8,128)(2,1)} %param.9) | copy-start | bytes 786436
  36.4 6.2 %copy-start.3 = (bf16[1,256,512]{2,1,0:T(8,128)(2,1)S(1)}, bf16[1,256,512]{2,1,0:T(8,128)(2,1)}, u32[]{:S(2)}) copy-start(bf16[1,256,512]{2,1,0:T(8,128)(2,1)} %param.10) | copy-start | bytes 786436
  42.5 0.9 %copy-start.7 = (bf16[64,2048]{1,0:T(8,128)(2,1)}, bf16[64,2048]{1,0:T(8,128)(2,1)S(1)}, u32[]{:S(2)}) copy-start(bf16[64,2048]{1,0:T(8,128)(2,1)S(1)} %constant_dynamic-update-slice_fusion) | copy-start | bytes 786436
  (3 other events, 1.9 us)

commit v2 on v1

--- a/solution.py
+++ b/solution.py
@@ -40,6 +40,7 @@
         out_specs=jax.tree.map(lambda _: VMEM, out_shape),
         scratch_shapes=scratch,
         name=name,
+        compiler_params=pltpu.CompilerParams(vmem_limit_bytes=16 << 20),
         cost_estimate=pl.CostEstimate(flops=flops, bytes_accessed=moved, transcendentals=0),
     )(*operands)
 

time: 43.7 us -> 33.8 us (0.77)
  Pallas kernels: 12.4 us -> 4.83 us
  local copies, waits for them, and re-layouts: 1.48 us -> 0.11 us
  other arithmetic: 3.06 us -> 2.25 us
    pallas_call x3, Pallas kernels: 12.4 us -> 4.83 us  [call(): pl.pallas_call(kernel, out_shape=out_shape, in_specs=[SMEM if o.dtype ==...]
    unnamed x42 -> x12, local copies, waits for them, and re-layouts: 1.4 us -> 0.03 us
    convert_element_type x1, other arithmetic: 0.85 us -> 0.05 us  [body(): old_other.astype(F32)]
  transfers between devices with their start and end apart: 14 -> 14, of which waited for: 4 -> 5; matrix products, arithmetic and copies ran while one was open for 2% -> 0% of each run, Pallas kernels for 7% -> 0%
where the time goes in v2:
time: 33.8 us; the launch traced here: 33.6 us
  starting transfers between devices  16.4 us (49%)
  waiting for transfers between devices  8.59 us (25%)
  Pallas kernels  4.83 us (14%)
  other arithmetic  2.25 us (7%)
  between operations  1.47 us (4%)
    ppermute x3, starting transfers between devices, body(): lax.ppermute(pieces[step], 'bcol', chip_pairs(step))  10.1 us
    ppermute x3, waiting for transfers between devices, body(): lax.ppermute(updates[step], 'bcol', chip_pairs(step))  5.98 us
    pallas_call x3, Pallas kernels, call(): pl.pallas_call(kernel, out_shape=out_shape, in_specs=[SMEM if o.dtype ==...  4.83 us
    ppermute x3, starting transfers between devices, body(): lax.ppermute(updates[step], 'bcol', chip_pairs(step))  4.41 us
    ppermute x3, waiting for transfers between devices, body(): lax.ppermute(pieces[step], 'bcol', chip_pairs(step))  2.33 us
    convert_element_type x1, other arithmetic, body(): given_stat = jnp.where(is_second, left_old, right_old).astype(BF16)  1.34 us
    ppermute x3, starting transfers between devices, body(): lax.ppermute(x, 'bcol', core_pairs())  1.07 us
    broadcast_in_dim x1, other arithmetic, body(): right_out[None]  0.85 us
  transfers between devices with their start and end apart: 14, of which 5 were waited for; matrix products, arithmetic and copies ran while one was open for 0% of the time, Pallas kernels for 0%

profile of v2, /device:TPU:0, one launch (start us, length us, event | category | flops | bytes accessed | tf_op | source)
XLA Modules:
  0.0 33.6 jit_solution(2495997531344236641)
XLA Ops:
  0.7 1.3 %select_convert_fusion = bf16[256,512]{1,0:T(8,128)(2,1)S(1)} fusion(pred[]{:T(512)S(6)} %eq.9, f32[1,256,512]{2,1,0:T(8,128)} %param.8, f32[1,256,512]{2,1,0:T(8,128)} %param.7), kind=kLoop, calls=%fused_computation | loop fusion | flops 131072 | bytes 1310721 | tf_op jit(solution)/shard_map/convert_element_type | solution.py:140
  2.0 0.6 %collective-permute-start.9 = (bf16[256,512]{1,0:T(8,128)(2,1)S(1)}, bf16[256,512]{1,0:T(8,128)(2,1)S(1)}, u32[]{:S(2)}, u32[]{:S(2)}) collective-permute-start(bf16[256,512]{1,0:T(8,128)(2,1)S(1)} %select_convert_fusion), channel_id=1, source_target_pairs={{0,1},{1,0},{2,3},{3,2},{4,5},{5,4},{6,7},{7,6},{8,9},{9,8},{10,11... | collective-permute-start | bytes 786440 | tf_op jit(solution)/shard_map/ppermute | solution.py:142
  2.6 0.1 collective-permute-start.7
  2.7 0.4 %collective-permute-start.8 = (bf16[256,512]{1,0:T(8,128)(2,1)S(1)}, bf16[256,512]{1,0:T(8,128)(2,1)S(1)}, u32[]{:S(2)}, u32[]{:S(2)}) collective-permute-start(bf16[256,512]{1,0:T(8,128)(2,1)S(1)} %bitcast.24), channel_id=1, source_target_pairs={{0,1},{1,0},{2,3},{3,2},{4,5},{5,4},{6,7},{7,6},{8,9},{9,8},{10,11... | collective-permute-start | bytes 786440 | tf_op jit(solution)/shard_map/ppermute | solution.py:142
  3.1 0.0 copy-start
  3.1 2.7 %collective-permute-start = (bf16[64,512]{1,0:T(8,128)(2,1)S(1)}, bf16[64,512]{1,0:T(8,128)(2,1)S(1)}, u32[]{:S(2)}, u32[]{:S(2)}) collective-permute-start(bf16[64,512]{1,0:T(8,128)(2,1)S(1)} %get-tuple-element.32), channel_id=1, source_target_pairs={{0,2},{1,3},{2,0},{3,1},{4,6},{5,7},{6,4},{7,5},{8,10},{9,11},{10,... | collective-permute-start | bytes 196616 | tf_op jit(solution)/shard_map/ppermute | solution.py:139
  5.8 2.6 %collective-permute-start.1 = (bf16[64,512]{1,0:T(8,128)(2,1)S(1)}, bf16[64,512]{1,0:T(8,128)(2,1)S(1)}, u32[]{:S(2)}, u32[]{:S(2)}) collective-permute-start(bf16[64,512]{1,0:T(8,128)(2,1)S(1)} %get-tuple-element.34), channel_id=1, source_target_pairs={{0,4},{1,5},{2,6},{3,7},{4,0},{5,1},{6,2},{7,3},{8,12},{9,13},{10,... | collective-permute-start | bytes 196616 | tf_op jit(solution)/shard_map/ppermute | solution.py:139
  8.4 0.1 collective-permute-done.refs_1_
  8.5 4.8 %collective-permute-start.2 = (bf16[64,512]{1,0:T(8,128)(2,1)S(1)}, bf16[64,512]{1,0:T(8,128)(2,1)S(1)}, u32[]{:S(2)}, u32[]{:S(2)}) collective-permute-start(bf16[64,512]{1,0:T(8,128)(2,1)S(1)} %get-tuple-element.31), channel_id=1, source_target_pairs={{0,6},{1,7},{2,4},{3,5},{4,2},{5,3},{6,0},{7,1},{8,14},{9,15},{10,... | collective-permute-start | bytes 196616 | tf_op jit(solution)/shard_map/ppermute | solution.py:139
  13.3 0.0 collective-permute-start.3
  13.3 2.2 %collective-permute-done.2.refs_3_ = bf16[64,512]{1,0:T(8,128)(2,1)S(1)} collective-permute-done((bf16[64,512]{1,0:T(8,128)(2,1)S(1)}, bf16[64,512]{1,0:T(8,128)(2,1)S(1)}, u32[]{:S(2)}, u32[]{:S(2)}) %collective-permute-start.2) | collective-permute-done | bytes 65568 | tf_op jit(solution)/shard_map/ppermute | solution.py:139
  15.5 0.0 collective-permute-start.4
  15.5 0.0 collective-permute-done.9
  15.5 0.5 %collective-permute-start.5 = (bf16[64,512]{1,0:T(8,128)(2,1)S(1)}, bf16[64,512]{1,0:T(8,128)(2,1)S(1)}, u32[]{:S(2)}, u32[]{:S(2)}) collective-permute-start(bf16[64,512]{1,0:T(8,128)(2,1)S(1)} %collective-permute-done.1.refs_2_), channel_id=1, source_target_pairs={{0,1},{1,0},{2,3},{3,2},{4,5},{5,4},{6,7},{7,6},{8,9},{9,8},{10,11... | collective-permute-start | bytes 196616 | tf_op jit(solution)/shard_map/ppermute | solution.py:144
  16.0 0.0 collective-permute-done.7.refs_1_
  16.0 0.1 collective-permute-start.6
  16.8 0.1 convert_element_type.7.refs_6_
  16.8 0.0 collective-permute-done.8.refs_3_
  16.9 0.1 prepare.1
  17.0 0.0 collective-permute-done.4.refs_5_
  17.0 0.0 collective-permute-done.5.refs_6_
  17.0 0.3 collective-permute-done.6.refs_7_
  17.3 0.7 %precondition.1 = (bf16[64,512]{1,0:T(8,128)(2,1)S(1)}, bf16[64,512]{1,0:T(8,128)(2,1)S(1)}, bf16[64,512]{1,0:T(8,128)(2,1)S(1)}, bf16[64,512]{1,0:T(8,128)(2,1)S(1)}, bf16[512,512]{1,0:T(8,128)(2,1)S(1)}) custom-call(bf16[64,512]{1,0:T(8,128)(2,1)S(1)} %get-tuple-element.33.refs_0_, bf16[64,512]{1,0:T(8,128)(2,1)S(1)} %collective-permute-done.refs_1_, ...), custom_call_target="tpu_custom_call" | custom-call | flops 402653184 | bytes 2097152 | tf_op jit(solution)/shard_map/precondition/pallas_call | solution.py:36
  18.0 4.0 %refreshed.1 = (f32[256,512]{1,0:T(8,128)}, f32[256,512]{1,0:T(8,128)}, bf16[256,512]{1,0:T(8,128)(2,1)S(1)}, bf16[256,512]{1,0:T(8,128)(2,1)S(1)}) custom-call(bf16[512,512]{1,0:T(8,128)(2,1)S(1)} %get-tuple-element.23.refs_0_, f32[256,512]{1,0:T(8,128)S(1)} %bitcast.19, f32[256,512]{1,0:T(8,128)S(1)} %bitcast.21, f32[512,512]{1,0:T(8,128)S(1)} %get-tuple-element.24.refs_3_), custom_call_target="tpu_custom_call" | custom-call | flops 2684354560 | bytes 8388608 | tf_op jit(solution)/shard_map/refreshed/pallas_call | solution.py:36
  22.0 0.2 collective-permute-start.13
  22.2 0.0 collective-permute-start.10
  22.3 4.4 %collective-permute-start.11 = (bf16[64,512]{1,0:T(8,128)(2,1)S(1)}, bf16[64,512]{1,0:T(8,128)(2,1)S(1)}, u32[]{:S(2)}, u32[]{:S(2)}) collective-permute-start(bf16[64,512]{1,0:T(8,128)(2,1)S(1)} %get-tuple-element.21), channel_id=1, source_target_pairs={{0,4},{1,5},{2,6},{3,7},{4,0},{5,1},{6,2},{7,3},{8,12},{9,13},{10,... | collective-permute-start | bytes 196616 | tf_op jit(solution)/shard_map/ppermute | solution.py:166
  26.7 0.0 collective-permute-done.10
  26.7 4.1 %collective-permute-done.11 = bf16[64,512]{1,0:T(8,128)(2,1)S(1)} collective-permute-done((bf16[64,512]{1,0:T(8,128)(2,1)S(1)}, bf16[64,512]{1,0:T(8,128)(2,1)S(1)}, u32[]{:S(2)}, u32[]{:S(2)}) %collective-permute-start.11) | collective-permute-done | bytes 65568 | tf_op jit(solution)/shard_map/ppermute | solution.py:166
  30.8 1.9 %collective-permute-done.12 = bf16[64,512]{1,0:T(8,128)(2,1)S(1)} collective-permute-done((bf16[64,512]{1,0:T(8,128)(2,1)S(1)}, bf16[64,512]{1,0:T(8,128)(2,1)S(1)}, u32[]{:S(2)}, u32[]{:S(2)}) %collective-permute-start.12) | collective-permute-done | bytes 65568 | tf_op jit(solution)/shard_map/ppermute | solution.py:166
  32.7 0.0 copy-start.5
  32.8 0.9 %select_bitcast_fusion = (bf16[1,256,512]{2,1,0:T(8,128)(2,1)}, bf16[1,256,512]{2,1,0:T(8,128)(2,1)}) fusion(bf16[256,512]{1,0:T(8,128)(2,1)S(1)} %get-tuple-element.28, bf16[256,512]{1,0:T(8,128)(2,1)S(1)} %collective-permute-done.13, pred[]{:T(512)} %bitcast.8, pred[]{:T(512)S(6)} %eq.9, bf16[1,256,512]{2,1,0:T(8,128)(2,1)S(1)} %copy-done.3, ...), kind=kLoop, calls=%fused_computation.1 | loop fusion | flops 524288 | bytes 1572866 | tf_op jit(solution)/shard_map/broadcast_in_dim | solution.py:181
  (20 shorter events, 0.1 us)
Async XLA Ops:
  0.6 1.9 %copy-start.2 = (bf16[1,256,512]{2,1,0:T(8,128)(2,1)S(1)}, bf16[1,256,512]{2,1,0:T(8,128)(2,1)}, u32[]{:S(2)}) copy-start(bf16[1,256,512]{2,1,0:T(8,128)(2,1)} %param.9) | copy-start | bytes 786436
  0.6 2.0 %copy-start.3 = (bf16[1,256,512]{2,1,0:T(8,128)(2,1)S(1)}, bf16[1,256,512]{2,1,0:T(8,128)(2,1)}, u32[]{:S(2)}) copy-start(bf16[1,256,512]{2,1,0:T(8,128)(2,1)} %param.10) | copy-start | bytes 786436
  0.7 2.4 %copy-start.4 = (bf16[64,2048]{1,0:T(8,128)(2,1)S(1)}, bf16[64,2048]{1,0:T(8,128)(2,1)}, u32[]{:S(2)}) copy-start(bf16[64,2048]{1,0:T(8,128)(2,1)} %param.6) | copy-start | bytes 786436
  2.0 13.5 %collective-permute-start.9 = (bf16[256,512]{1,0:T(8,128)(2,1)S(1)}, bf16[256,512]{1,0:T(8,128)(2,1)S(1)}, u32[]{:S(2)}, u32[]{:S(2)}) collective-permute-start(bf16[256,512]{1,0:T(8,128)(2,1)S(1)} %select_convert_fusion), channel_id=1, source_target_pairs={{0,1},{1,0},{2,3},{3,2},{4,5},{5,4},{6,7},{7,6},{8,9},{9,8},{10,11... | collective-permute-start | bytes 786440 | tf_op jit(solution)/shard_map/ppermute | solution.py:142
  2.6 13.5 %collective-permute-start.7 = (bf16[256,512]{1,0:T(8,128)(2,1)S(1)}, bf16[256,512]{1,0:T(8,128)(2,1)S(1)}, u32[]{:S(2)}, u32[]{:S(2)}) collective-permute-start(bf16[256,512]{1,0:T(8,128)(2,1)S(1)} %bitcast.22), channel_id=1, source_target_pairs={{0,1},{1,0},{2,3},{3,2},{4,5},{5,4},{6,7},{7,6},{8,9},{9,8},{10,11... | collective-permute-start | bytes 786440 | tf_op jit(solution)/shard_map/ppermute | solution.py:142
  2.7 14.2 %collective-permute-start.8 = (bf16[256,512]{1,0:T(8,128)(2,1)S(1)}, bf16[256,512]{1,0:T(8,128)(2,1)S(1)}, u32[]{:S(2)}, u32[]{:S(2)}) collective-permute-start(bf16[256,512]{1,0:T(8,128)(2,1)S(1)} %bitcast.24), channel_id=1, source_target_pairs={{0,1},{1,0},{2,3},{3,2},{4,5},{5,4},{6,7},{7,6},{8,9},{9,8},{10,11... | collective-permute-start | bytes 786440 | tf_op jit(solution)/shard_map/ppermute | solution.py:142
  3.1 13.7 %copy-start.1 = (f32[1,256,512]{2,1,0:T(8,128)S(1)}, f32[1,256,512]{2,1,0:T(8,128)}, u32[]{:S(2)}) copy-start(f32[1,256,512]{2,1,0:T(8,128)} %param.8) | copy-start | bytes 1572868
  3.1 13.7 %copy-start = (f32[1,256,512]{2,1,0:T(8,128)S(1)}, f32[1,256,512]{2,1,0:T(8,128)}, u32[]{:S(2)}) copy-start(f32[1,256,512]{2,1,0:T(8,128)} %param.7) | copy-start | bytes 1572868
  3.1 5.4 %collective-permute-start = (bf16[64,512]{1,0:T(8,128)(2,1)S(1)}, bf16[64,512]{1,0:T(8,128)(2,1)S(1)}, u32[]{:S(2)}, u32[]{:S(2)}) collective-permute-start(bf16[64,512]{1,0:T(8,128)(2,1)S(1)} %get-tuple-element.32), channel_id=1, source_target_pairs={{0,2},{1,3},{2,0},{3,1},{4,6},{5,7},{6,4},{7,5},{8,10},{9,11},{10,... | collective-permute-start | bytes 196616 | tf_op jit(solution)/shard_map/ppermute | solution.py:139
  5.8 7.4 %collective-permute-start.1 = (bf16[64,512]{1,0:T(8,128)(2,1)S(1)}, bf16[64,512]{1,0:T(8,128)(2,1)S(1)}, u32[]{:S(2)}, u32[]{:S(2)}) collective-permute-start(bf16[64,512]{1,0:T(8,128)(2,1)S(1)} %get-tuple-element.34), channel_id=1, source_target_pairs={{0,4},{1,5},{2,6},{3,7},{4,0},{5,1},{6,2},{7,3},{8,12},{9,13},{10,... | collective-permute-start | bytes 196616 | tf_op jit(solution)/shard_map/ppermute | solution.py:139
  8.5 7.0 %collective-permute-start.2 = (bf16[64,512]{1,0:T(8,128)(2,1)S(1)}, bf16[64,512]{1,0:T(8,128)(2,1)S(1)}, u32[]{:S(2)}, u32[]{:S(2)}) collective-permute-start(bf16[64,512]{1,0:T(8,128)(2,1)S(1)} %get-tuple-element.31), channel_id=1, source_target_pairs={{0,6},{1,7},{2,4},{3,5},{4,2},{5,3},{6,0},{7,1},{8,14},{9,15},{10,... | collective-permute-start | bytes 196616 | tf_op jit(solution)/shard_map/ppermute | solution.py:139
  13.3 3.7 %collective-permute-start.3 = (bf16[64,512]{1,0:T(8,128)(2,1)S(1)}, bf16[64,512]{1,0:T(8,128)(2,1)S(1)}, u32[]{:S(2)}, u32[]{:S(2)}) collective-permute-start(bf16[64,512]{1,0:T(8,128)(2,1)S(1)} %get-tuple-element.33.refs_0_), channel_id=1, source_target_pairs={{0,1},{1,0},{2,3},{3,2},{4,5},{5,4},{6,7},{7,6},{8,9},{9,8},{10,11... | collective-permute-start | bytes 196616 | tf_op jit(solution)/shard_map/ppermute | solution.py:144
  15.5 1.5 %collective-permute-start.4 = (bf16[64,512]{1,0:T(8,128)(2,1)S(1)}, bf16[64,512]{1,0:T(8,128)(2,1)S(1)}, u32[]{:S(2)}, u32[]{:S(2)}) collective-permute-start(bf16[64,512]{1,0:T(8,128)(2,1)S(1)} %collective-permute-done.refs_1_), channel_id=1, source_target_pairs={{0,1},{1,0},{2,3},{3,2},{4,5},{5,4},{6,7},{7,6},{8,9},{9,8},{10,11... | collective-permute-start | bytes 196616 | tf_op jit(solution)/shard_map/ppermute | solution.py:144
  15.5 1.5 %collective-permute-start.5 = (bf16[64,512]{1,0:T(8,128)(2,1)S(1)}, bf16[64,512]{1,0:T(8,128)(2,1)S(1)}, u32[]{:S(2)}, u32[]{:S(2)}) collective-permute-start(bf16[64,512]{1,0:T(8,128)(2,1)S(1)} %collective-permute-done.1.refs_2_), channel_id=1, source_target_pairs={{0,1},{1,0},{2,3},{3,2},{4,5},{5,4},{6,7},{7,6},{8,9},{9,8},{10,11... | collective-permute-start | bytes 196616 | tf_op jit(solution)/shard_map/ppermute | solution.py:144
  16.0 1.3 %collective-permute-start.6 = (bf16[64,512]{1,0:T(8,128)(2,1)S(1)}, bf16[64,512]{1,0:T(8,128)(2,1)S(1)}, u32[]{:S(2)}, u32[]{:S(2)}) collective-permute-start(bf16[64,512]{1,0:T(8,128)(2,1)S(1)} %collective-permute-done.2.refs_3_), channel_id=1, source_target_pairs={{0,1},{1,0},{2,3},{3,2},{4,5},{5,4},{6,7},{7,6},{8,9},{9,8},{10,11... | collective-permute-start | bytes 196616 | tf_op jit(solution)/shard_map/ppermute | solution.py:144
  22.0 10.7 %collective-permute-start.13 = (bf16[256,512]{1,0:T(8,128)(2,1)S(1)}, bf16[256,512]{1,0:T(8,128)(2,1)S(1)}, u32[]{:S(2)}, u32[]{:S(2)}) collective-permute-start(bf16[256,512]{1,0:T(8,128)(2,1)S(1)} %get-tuple-element.27), channel_id=1, source_target_pairs={{0,1},{1,0},{2,3},{3,2},{4,5},{5,4},{6,7},{7,6},{8,9},{9,8},{10,11... | collective-permute-start | bytes 786440 | tf_op jit(solution)/shard_map/ppermute | solution.py:174
  22.2 4.5 %collective-permute-start.10 = (bf16[64,512]{1,0:T(8,128)(2,1)S(1)}, bf16[64,512]{1,0:T(8,128)(2,1)S(1)}, u32[]{:S(2)}, u32[]{:S(2)}) collective-permute-start(bf16[64,512]{1,0:T(8,128)(2,1)S(1)} %get-tuple-element.20), channel_id=1, source_target_pairs={{0,2},{1,3},{2,0},{3,1},{4,6},{5,7},{6,4},{7,5},{8,10},{9,11},{10,... | collective-permute-start | bytes 196616 | tf_op jit(solution)/shard_map/ppermute | solution.py:166
  22.3 8.5 %collective-permute-start.11 = (bf16[64,512]{1,0:T(8,128)(2,1)S(1)}, bf16[64,512]{1,0:T(8,128)(2,1)S(1)}, u32[]{:S(2)}, u32[]{:S(2)}) collective-permute-start(bf16[64,512]{1,0:T(8,128)(2,1)S(1)} %get-tuple-element.21), channel_id=1, source_target_pairs={{0,4},{1,5},{2,6},{3,7},{4,0},{5,1},{6,2},{7,3},{8,12},{9,13},{10,... | collective-permute-start | bytes 196616 | tf_op jit(solution)/shard_map/ppermute | solution.py:166
  26.7 6.1 %collective-permute-start.12 = (bf16[64,512]{1,0:T(8,128)(2,1)S(1)}, bf16[64,512]{1,0:T(8,128)(2,1)S(1)}, u32[]{:S(2)}, u32[]{:S(2)}) collective-permute-start(bf16[64,512]{1,0:T(8,128)(2,1)S(1)} %get-tuple-element.22), channel_id=1, source_target_pairs={{0,6},{1,7},{2,4},{3,5},{4,2},{5,3},{6,0},{7,1},{8,14},{9,15},{10,... | collective-permute-start | bytes 196616 | tf_op jit(solution)/shard_map/ppermute | solution.py:166
  32.7 0.9 %copy-start.5 = (bf16[64,2048]{1,0:T(8,128)(2,1)}, bf16[64,2048]{1,0:T(8,128)(2,1)S(1)}, u32[]{:S(2)}) copy-start(bf16[64,2048]{1,0:T(8,128)(2,1)S(1)} %constant_dynamic-update-slice_fusion) | copy-start | bytes 786436

commit v3 on v2

--- a/solution.py
+++ b/solution.py
@@ -27,22 +27,29 @@
     return [(i, i ^ 1) for i in range(lax.axis_size("bcol"))]
 
 
+def permute(value, pairs):
+    return lax.ppermute(value, "bcol", pairs)
+
+
 def dot(left_side, right_side, contract=((1,), (0,))):
     return lax.dot_general(left_side, right_side, (contract, ((), ())), preferred_element_type=F32)
 
 
-def call(kernel, out_shape, scratch, cost, name):
+def call(kernel, out_shape, scratch, cost):
     flops, moved = cost
-    return lambda *operands: pl.pallas_call(
+
+    def run(*operands):
+      return pl.pallas_call(
         kernel,
         out_shape=out_shape,
         in_specs=[SMEM if o.dtype == jnp.int32 else VMEM for o in operands],
         out_specs=jax.tree.map(lambda _: VMEM, out_shape),
         scratch_shapes=scratch,
-        name=name,
         compiler_params=pltpu.CompilerParams(vmem_limit_bytes=16 << 20),
         cost_estimate=pl.CostEstimate(flops=flops, bytes_accessed=moved, transcendentals=0),
     )(*operands)
+
+    return run
 
 
 def prepare(chips, rows, order, left_mine, left_other, right_mine, right_other, old_left, old_right, old_other,
@@ -77,7 +84,7 @@
 
 
 def refreshed(order, whole, old_left, old_right, old_side, new_left, new_right, root_mine, root_other, stat, weight, root):
-    column, half = place()
+    _, half = place()
     span = order // 2
     mine = pl.ds(pl.multiple_of(half * span, span), span)
     other = pl.ds(pl.multiple_of((1 - half) * span, span), span)
@@ -105,7 +112,7 @@
     held = 1.25
     weight[...] = -0.25 * stat[...]
     square = 25.0 / 16.0
-    for iteration in range(1, ITERS):
+    for _ in range(1, ITERS):
         moment = stat[...]
         narrow = moment.astype(BF16)
         change = (dot(narrow, narrow) - 10.0 * moment) * (1.0 / 16.0)
@@ -122,7 +129,7 @@
     root_other[...] = root[other, :]
 
 
-def body(gradient, left_stats, right_stats, left_roots, right_roots, refresh):
+def step(gradient, left_stats, right_stats, left_roots, right_roots, refresh):
     column, half = place()
     chips = lax.axis_size("bcol") // 2
     rows = gradient.shape[0]
@@ -136,12 +143,10 @@
         return lax.dynamic_slice(gradient, (0, (column ^ step) * order), (rows, order))
 
     pieces = [piece(step) for step in range(chips)]
-    mine = [pieces[0]] + [lax.ppermute(pieces[step], "bcol", chip_pairs(step)) for step in range(1, chips)]
+    mine = [pieces[0]] + [permute(pieces[step], chip_pairs(step)) for step in range(1, chips)]
     given_stat = jnp.where(is_second, left_old, right_old).astype(BF16)
-    left_other, right_other, old_other = [
-        lax.ppermute(x, "bcol", core_pairs()) for x in (left_root, right_root, given_stat)
-    ]
-    other = [lax.ppermute(x, "bcol", core_pairs()) for x in mine]
+    left_other, right_other, old_other = [permute(x, core_pairs()) for x in (left_root, right_root, given_stat)]
+    other = [permute(x, core_pairs()) for x in mine]
 
     def shape(r, c, t):
         return jax.ShapeDtypeStruct((r, c), t)
@@ -154,24 +159,21 @@
         (shape(span, order, BF16), shape(order, order, BF16), shape(order, order, F32)),
         [pltpu.VMEM((order, order), BF16)],
         (0, 4 * order * order * 2),
-        "prepare",
     )(left_root, left_other, right_root, right_other, left_old, right_old, old_other.astype(F32))
     *updates, whole = call(
         kernel(precondition, chips, rows, order),
         (*[shape(rows, order, BF16)] * chips, shape(order, order, BF16)),
         [],
         (3 * order**3, 4 * order * order * 2),
-        "precondition",
     )(*mine, *other, left_rows, right_full)
-    returned = [updates[0]] + [lax.ppermute(updates[step], "bcol", chip_pairs(step)) for step in range(1, chips)]
+    returned = [updates[0]] + [permute(updates[step], chip_pairs(step)) for step in range(1, chips)]
     left_new, right_new, root_mine, root_other = call(
         kernel(refreshed, order),
         (shape(span, order, F32), shape(span, order, F32), shape(span, order, BF16), shape(span, order, BF16)),
         [pltpu.VMEM((order, order), F32), pltpu.VMEM((order, order), F32), pltpu.VMEM((order, order), BF16)],
         (20 * order**3, 8 * order * order * 4),
-        "refreshed",
     )(whole, left_old, right_old, old_side)
-    taken = lax.ppermute(root_other, "bcol", core_pairs())
+    taken = permute(root_other, core_pairs())
     listed = jnp.any(refresh[0] == column)
     left_out = jnp.where(listed, jnp.where(is_second, taken, root_mine), left_root)
     right_out = jnp.where(listed, jnp.where(is_second, root_mine, taken), right_root)
@@ -186,4 +188,4 @@
     rows = P(("brow", "bcol"), None)
     in_specs = (rows, block, block, block, block, P("brow", None))
     out_specs = (rows, block, block, block, block)
-    return jax.shard_map(body, mesh=mesh, in_specs=in_specs, out_specs=out_specs, check_vma=False)
+    return jax.shard_map(step, mesh=mesh, in_specs=in_specs, out_specs=out_specs, check_vma=False)

time: 33.8 us -> 33.8 us (level)
  no operation moved by 1% of the time
where the time goes in v3:
time: 33.8 us; the launch traced here: 33.6 us
  starting transfers between devices  16.4 us (49%)
  waiting for transfers between devices  8.59 us (25%)
  Pallas kernels  4.83 us (14%)
  other arithmetic  2.25 us (7%)
  between operations  1.47 us (4%)
    ppermute x14, starting transfers between devices, permute(): return lax.ppermute(value, 'bcol', pairs)  16.4 us
    ppermute x14, waiting for transfers between devices, permute(): return lax.ppermute(value, 'bcol', pairs)  8.59 us
    pallas_call x3, Pallas kernels, run(): pl.pallas_call(kernel, out_shape=out_shape, in_specs=[SMEM if o.dtype ==...  4.83 us
    convert_element_type x1, other arithmetic, step(): given_stat = jnp.where(is_second, left_old, right_old).astype(BF16)  1.34 us
    broadcast_in_dim x1, other arithmetic, step(): right_out[None]  0.85 us
  transfers between devices with their start and end apart: 14, of which 5 were waited for; matrix products, arithmetic and copies ran while one was open for 0% of the time, Pallas kernels for 0%

profile of v3, /device:TPU:0, one launch (start us, length us, event | category | flops | bytes accessed | tf_op | source)
XLA Modules:
  0.0 33.6 jit_solution(2495997531344236641)
XLA Ops:
  0.7 1.3 %select_convert_fusion = bf16[256,512]{1,0:T(8,128)(2,1)S(1)} fusion(pred[]{:T(512)S(6)} %eq.9, f32[1,256,512]{2,1,0:T(8,128)} %param.8, f32[1,256,512]{2,1,0:T(8,128)} %param.7), kind=kLoop, calls=%fused_computation | loop fusion | flops 131072 | bytes 1310721 | tf_op jit(solution)/shard_map/convert_element_type | solution.py:147
  2.0 0.6 %collective-permute-start.9 = (bf16[256,512]{1,0:T(8,128)(2,1)S(1)}, bf16[256,512]{1,0:T(8,128)(2,1)S(1)}, u32[]{:S(2)}, u32[]{:S(2)}) collective-permute-start(bf16[256,512]{1,0:T(8,128)(2,1)S(1)} %select_convert_fusion), channel_id=1, source_target_pairs={{0,1},{1,0},{2,3},{3,2},{4,5},{5,4},{6,7},{7,6},{8,9},{9,8},{10,11... | collective-permute-start | bytes 786440 | tf_op jit(solution)/shard_map/ppermute | solution.py:31
  2.6 0.1 collective-permute-start.7
  2.7 0.4 %collective-permute-start.8 = (bf16[256,512]{1,0:T(8,128)(2,1)S(1)}, bf16[256,512]{1,0:T(8,128)(2,1)S(1)}, u32[]{:S(2)}, u32[]{:S(2)}) collective-permute-start(bf16[256,512]{1,0:T(8,128)(2,1)S(1)} %bitcast.24), channel_id=1, source_target_pairs={{0,1},{1,0},{2,3},{3,2},{4,5},{5,4},{6,7},{7,6},{8,9},{9,8},{10,11... | collective-permute-start | bytes 786440 | tf_op jit(solution)/shard_map/ppermute | solution.py:31
  3.1 0.0 copy-start
  3.1 2.7 %collective-permute-start = (bf16[64,512]{1,0:T(8,128)(2,1)S(1)}, bf16[64,512]{1,0:T(8,128)(2,1)S(1)}, u32[]{:S(2)}, u32[]{:S(2)}) collective-permute-start(bf16[64,512]{1,0:T(8,128)(2,1)S(1)} %get-tuple-element.32), channel_id=1, source_target_pairs={{0,2},{1,3},{2,0},{3,1},{4,6},{5,7},{6,4},{7,5},{8,10},{9,11},{10,... | collective-permute-start | bytes 196616 | tf_op jit(solution)/shard_map/ppermute | solution.py:31
  5.8 2.6 %collective-permute-start.1 = (bf16[64,512]{1,0:T(8,128)(2,1)S(1)}, bf16[64,512]{1,0:T(8,128)(2,1)S(1)}, u32[]{:S(2)}, u32[]{:S(2)}) collective-permute-start(bf16[64,512]{1,0:T(8,128)(2,1)S(1)} %get-tuple-element.34), channel_id=1, source_target_pairs={{0,4},{1,5},{2,6},{3,7},{4,0},{5,1},{6,2},{7,3},{8,12},{9,13},{10,... | collective-permute-start | bytes 196616 | tf_op jit(solution)/shard_map/ppermute | solution.py:31
  8.4 0.1 collective-permute-done.refs_1_
  8.5 4.8 %collective-permute-start.2 = (bf16[64,512]{1,0:T(8,128)(2,1)S(1)}, bf16[64,512]{1,0:T(8,128)(2,1)S(1)}, u32[]{:S(2)}, u32[]{:S(2)}) collective-permute-start(bf16[64,512]{1,0:T(8,128)(2,1)S(1)} %get-tuple-element.31), channel_id=1, source_target_pairs={{0,6},{1,7},{2,4},{3,5},{4,2},{5,3},{6,0},{7,1},{8,14},{9,15},{10,... | collective-permute-start | bytes 196616 | tf_op jit(solution)/shard_map/ppermute | solution.py:31
  13.3 0.0 collective-permute-done.1.refs_2_
  13.3 0.0 collective-permute-start.3
  13.3 2.2 %collective-permute-done.2.refs_3_ = bf16[64,512]{1,0:T(8,128)(2,1)S(1)} collective-permute-done((bf16[64,512]{1,0:T(8,128)(2,1)S(1)}, bf16[64,512]{1,0:T(8,128)(2,1)S(1)}, u32[]{:S(2)}, u32[]{:S(2)}) %collective-permute-start.2) | collective-permute-done | bytes 65568 | tf_op jit(solution)/shard_map/ppermute | solution.py:31
  15.5 0.0 collective-permute-start.4
  15.5 0.0 collective-permute-done.9
  15.5 0.5 %collective-permute-start.5 = (bf16[64,512]{1,0:T(8,128)(2,1)S(1)}, bf16[64,512]{1,0:T(8,128)(2,1)S(1)}, u32[]{:S(2)}, u32[]{:S(2)}) collective-permute-start(bf16[64,512]{1,0:T(8,128)(2,1)S(1)} %collective-permute-done.1.refs_2_), channel_id=1, source_target_pairs={{0,1},{1,0},{2,3},{3,2},{4,5},{5,4},{6,7},{7,6},{8,9},{9,8},{10,11... | collective-permute-start | bytes 196616 | tf_op jit(solution)/shard_map/ppermute | solution.py:31
  16.0 0.0 collective-permute-done.7.refs_1_
  16.0 0.1 collective-permute-start.6
  16.8 0.1 convert_element_type.7.refs_6_
  16.8 0.0 collective-permute-done.8.refs_3_
  16.9 0.1 shard_map.101
  17.0 0.0 collective-permute-done.3.refs_4_
  17.0 0.0 collective-permute-done.4.refs_5_
  17.0 0.3 collective-permute-done.6.refs_7_
  17.3 0.7 %shard_map.102 = (bf16[64,512]{1,0:T(8,128)(2,1)S(1)}, bf16[64,512]{1,0:T(8,128)(2,1)S(1)}, bf16[64,512]{1,0:T(8,128)(2,1)S(1)}, bf16[64,512]{1,0:T(8,128)(2,1)S(1)}, bf16[512,512]{1,0:T(8,128)(2,1)S(1)}) custom-call(bf16[64,512]{1,0:T(8,128)(2,1)S(1)} %get-tuple-element.33.refs_0_, bf16[64,512]{1,0:T(8,128)(2,1)S(1)} %collective-permute-done.refs_1_, ...), custom_call_target="tpu_custom_call" | custom-call | flops 402653184 | bytes 2097152 | tf_op jit(solution)/shard_map/pallas_call | solution.py:42
  18.0 4.0 %shard_map.103 = (f32[256,512]{1,0:T(8,128)}, f32[256,512]{1,0:T(8,128)}, bf16[256,512]{1,0:T(8,128)(2,1)S(1)}, bf16[256,512]{1,0:T(8,128)(2,1)S(1)}) custom-call(bf16[512,512]{1,0:T(8,128)(2,1)S(1)} %get-tuple-element.23.refs_0_, f32[256,512]{1,0:T(8,128)S(1)} %bitcast.19, f32[256,512]{1,0:T(8,128)S(1)} %bitcast.21, f32[512,512]{1,0:T(8,128)S(1)} %get-tuple-element.24.refs_3_), custom_call_target="tpu_custom_call" | custom-call | flops 2684354560 | bytes 8388608 | tf_op jit(solution)/shard_map/pallas_call | solution.py:42
  22.0 0.2 collective-permute-start.13
  22.3 4.4 %collective-permute-start.11 = (bf16[64,512]{1,0:T(8,128)(2,1)S(1)}, bf16[64,512]{1,0:T(8,128)(2,1)S(1)}, u32[]{:S(2)}, u32[]{:S(2)}) collective-permute-start(bf16[64,512]{1,0:T(8,128)(2,1)S(1)} %get-tuple-element.21), channel_id=1, source_target_pairs={{0,4},{1,5},{2,6},{3,7},{4,0},{5,1},{6,2},{7,3},{8,12},{9,13},{10,... | collective-permute-start | bytes 196616 | tf_op jit(solution)/shard_map/ppermute | solution.py:31
  26.7 0.0 collective-permute-start.12
  26.7 4.1 %collective-permute-done.11 = bf16[64,512]{1,0:T(8,128)(2,1)S(1)} collective-permute-done((bf16[64,512]{1,0:T(8,128)(2,1)S(1)}, bf16[64,512]{1,0:T(8,128)(2,1)S(1)}, u32[]{:S(2)}, u32[]{:S(2)}) %collective-permute-start.11) | collective-permute-done | bytes 65568 | tf_op jit(solution)/shard_map/ppermute | solution.py:31
  30.8 1.9 %collective-permute-done.12 = bf16[64,512]{1,0:T(8,128)(2,1)S(1)} collective-permute-done((bf16[64,512]{1,0:T(8,128)(2,1)S(1)}, bf16[64,512]{1,0:T(8,128)(2,1)S(1)}, u32[]{:S(2)}, u32[]{:S(2)}) %collective-permute-start.12) | collective-permute-done | bytes 65568 | tf_op jit(solution)/shard_map/ppermute | solution.py:31
  32.7 0.0 copy-start.5
  32.8 0.9 %select_bitcast_fusion = (bf16[1,256,512]{2,1,0:T(8,128)(2,1)}, bf16[1,256,512]{2,1,0:T(8,128)(2,1)}) fusion(bf16[256,512]{1,0:T(8,128)(2,1)S(1)} %get-tuple-element.28, bf16[256,512]{1,0:T(8,128)(2,1)S(1)} %collective-permute-done.13, pred[]{:T(512)} %bitcast.8, pred[]{:T(512)S(6)} %eq.9, bf16[1,256,512]{2,1,0:T(8,128)(2,1)S(1)} %copy-done.3, ...), kind=kLoop, calls=%fused_computation.1 | loop fusion | flops 524288 | bytes 1572866 | tf_op jit(solution)/shard_map/broadcast_in_dim | solution.py:183
  (20 shorter events, 0.1 us)
Async XLA Ops:
  0.6 1.9 %copy-start.2 = (bf16[1,256,512]{2,1,0:T(8,128)(2,1)S(1)}, bf16[1,256,512]{2,1,0:T(8,128)(2,1)}, u32[]{:S(2)}) copy-start(bf16[1,256,512]{2,1,0:T(8,128)(2,1)} %param.9) | copy-start | bytes 786436
  0.6 2.0 %copy-start.3 = (bf16[1,256,512]{2,1,0:T(8,128)(2,1)S(1)}, bf16[1,256,512]{2,1,0:T(8,128)(2,1)}, u32[]{:S(2)}) copy-start(bf16[1,256,512]{2,1,0:T(8,128)(2,1)} %param.10) | copy-start | bytes 786436
  0.7 2.4 %copy-start.4 = (bf16[64,2048]{1,0:T(8,128)(2,1)S(1)}, bf16[64,2048]{1,0:T(8,128)(2,1)}, u32[]{:S(2)}) copy-start(bf16[64,2048]{1,0:T(8,128)(2,1)} %param.6) | copy-start | bytes 786436
  2.0 13.5 %collective-permute-start.9 = (bf16[256,512]{1,0:T(8,128)(2,1)S(1)}, bf16[256,512]{1,0:T(8,128)(2,1)S(1)}, u32[]{:S(2)}, u32[]{:S(2)}) collective-permute-start(bf16[256,512]{1,0:T(8,128)(2,1)S(1)} %select_convert_fusion), channel_id=1, source_target_pairs={{0,1},{1,0},{2,3},{3,2},{4,5},{5,4},{6,7},{7,6},{8,9},{9,8},{10,11... | collective-permute-start | bytes 786440 | tf_op jit(solution)/shard_map/ppermute | solution.py:31
  2.6 13.5 %collective-permute-start.7 = (bf16[256,512]{1,0:T(8,128)(2,1)S(1)}, bf16[256,512]{1,0:T(8,128)(2,1)S(1)}, u32[]{:S(2)}, u32[]{:S(2)}) collective-permute-start(bf16[256,512]{1,0:T(8,128)(2,1)S(1)} %bitcast.22), channel_id=1, source_target_pairs={{0,1},{1,0},{2,3},{3,2},{4,5},{5,4},{6,7},{7,6},{8,9},{9,8},{10,11... | collective-permute-start | bytes 786440 | tf_op jit(solution)/shard_map/ppermute | solution.py:31
  2.7 14.2 %collective-permute-start.8 = (bf16[256,512]{1,0:T(8,128)(2,1)S(1)}, bf16[256,512]{1,0:T(8,128)(2,1)S(1)}, u32[]{:S(2)}, u32[]{:S(2)}) collective-permute-start(bf16[256,512]{1,0:T(8,128)(2,1)S(1)} %bitcast.24), channel_id=1, source_target_pairs={{0,1},{1,0},{2,3},{3,2},{4,5},{5,4},{6,7},{7,6},{8,9},{9,8},{10,11... | collective-permute-start | bytes 786440 | tf_op jit(solution)/shard_map/ppermute | solution.py:31
  3.1 13.7 %copy-start.1 = (f32[1,256,512]{2,1,0:T(8,128)S(1)}, f32[1,256,512]{2,1,0:T(8,128)}, u32[]{:S(2)}) copy-start(f32[1,256,512]{2,1,0:T(8,128)} %param.8) | copy-start | bytes 1572868
  3.1 13.7 %copy-start = (f32[1,256,512]{2,1,0:T(8,128)S(1)}, f32[1,256,512]{2,1,0:T(8,128)}, u32[]{:S(2)}) copy-start(f32[1,256,512]{2,1,0:T(8,128)} %param.7) | copy-start | bytes 1572868
  3.1 5.4 %collective-permute-start = (bf16[64,512]{1,0:T(8,128)(2,1)S(1)}, bf16[64,512]{1,0:T(8,128)(2,1)S(1)}, u32[]{:S(2)}, u32[]{:S(2)}) collective-permute-start(bf16[64,512]{1,0:T(8,128)(2,1)S(1)} %get-tuple-element.32), channel_id=1, source_target_pairs={{0,2},{1,3},{2,0},{3,1},{4,6},{5,7},{6,4},{7,5},{8,10},{9,11},{10,... | collective-permute-start | bytes 196616 | tf_op jit(solution)/shard_map/ppermute | solution.py:31
  5.8 7.4 %collective-permute-start.1 = (bf16[64,512]{1,0:T(8,128)(2,1)S(1)}, bf16[64,512]{1,0:T(8,128)(2,1)S(1)}, u32[]{:S(2)}, u32[]{:S(2)}) collective-permute-start(bf16[64,512]{1,0:T(8,128)(2,1)S(1)} %get-tuple-element.34), channel_id=1, source_target_pairs={{0,4},{1,5},{2,6},{3,7},{4,0},{5,1},{6,2},{7,3},{8,12},{9,13},{10,... | collective-permute-start | bytes 196616 | tf_op jit(solution)/shard_map/ppermute | solution.py:31
  8.5 7.0 %collective-permute-start.2 = (bf16[64,512]{1,0:T(8,128)(2,1)S(1)}, bf16[64,512]{1,0:T(8,128)(2,1)S(1)}, u32[]{:S(2)}, u32[]{:S(2)}) collective-permute-start(bf16[64,512]{1,0:T(8,128)(2,1)S(1)} %get-tuple-element.31), channel_id=1, source_target_pairs={{0,6},{1,7},{2,4},{3,5},{4,2},{5,3},{6,0},{7,1},{8,14},{9,15},{10,... | collective-permute-start | bytes 196616 | tf_op jit(solution)/shard_map/ppermute | solution.py:31
  13.3 3.7 %collective-permute-start.3 = (bf16[64,512]{1,0:T(8,128)(2,1)S(1)}, bf16[64,512]{1,0:T(8,128)(2,1)S(1)}, u32[]{:S(2)}, u32[]{:S(2)}) collective-permute-start(bf16[64,512]{1,0:T(8,128)(2,1)S(1)} %get-tuple-element.33.refs_0_), channel_id=1, source_target_pairs={{0,1},{1,0},{2,3},{3,2},{4,5},{5,4},{6,7},{7,6},{8,9},{9,8},{10,11... | collective-permute-start | bytes 196616 | tf_op jit(solution)/shard_map/ppermute | solution.py:31
  15.5 1.5 %collective-permute-start.4 = (bf16[64,512]{1,0:T(8,128)(2,1)S(1)}, bf16[64,512]{1,0:T(8,128)(2,1)S(1)}, u32[]{:S(2)}, u32[]{:S(2)}) collective-permute-start(bf16[64,512]{1,0:T(8,128)(2,1)S(1)} %collective-permute-done.refs_1_), channel_id=1, source_target_pairs={{0,1},{1,0},{2,3},{3,2},{4,5},{5,4},{6,7},{7,6},{8,9},{9,8},{10,11... | collective-permute-start | bytes 196616 | tf_op jit(solution)/shard_map/ppermute | solution.py:31
  15.5 1.5 %collective-permute-start.5 = (bf16[64,512]{1,0:T(8,128)(2,1)S(1)}, bf16[64,512]{1,0:T(8,128)(2,1)S(1)}, u32[]{:S(2)}, u32[]{:S(2)}) collective-permute-start(bf16[64,512]{1,0:T(8,128)(2,1)S(1)} %collective-permute-done.1.refs_2_), channel_id=1, source_target_pairs={{0,1},{1,0},{2,3},{3,2},{4,5},{5,4},{6,7},{7,6},{8,9},{9,8},{10,11... | collective-permute-start | bytes 196616 | tf_op jit(solution)/shard_map/ppermute | solution.py:31
  16.0 1.3 %collective-permute-start.6 = (bf16[64,512]{1,0:T(8,128)(2,1)S(1)}, bf16[64,512]{1,0:T(8,128)(2,1)S(1)}, u32[]{:S(2)}, u32[]{:S(2)}) collective-permute-start(bf16[64,512]{1,0:T(8,128)(2,1)S(1)} %collective-permute-done.2.refs_3_), channel_id=1, source_target_pairs={{0,1},{1,0},{2,3},{3,2},{4,5},{5,4},{6,7},{7,6},{8,9},{9,8},{10,11... | collective-permute-start | bytes 196616 | tf_op jit(solution)/shard_map/ppermute | solution.py:31
  22.0 10.7 %collective-permute-start.13 = (bf16[256,512]{1,0:T(8,128)(2,1)S(1)}, bf16[256,512]{1,0:T(8,128)(2,1)S(1)}, u32[]{:S(2)}, u32[]{:S(2)}) collective-permute-start(bf16[256,512]{1,0:T(8,128)(2,1)S(1)} %get-tuple-element.27), channel_id=1, source_target_pairs={{0,1},{1,0},{2,3},{3,2},{4,5},{5,4},{6,7},{7,6},{8,9},{9,8},{10,11... | collective-permute-start | bytes 786440 | tf_op jit(solution)/shard_map/ppermute | solution.py:31
  22.2 4.5 %collective-permute-start.10 = (bf16[64,512]{1,0:T(8,128)(2,1)S(1)}, bf16[64,512]{1,0:T(8,128)(2,1)S(1)}, u32[]{:S(2)}, u32[]{:S(2)}) collective-permute-start(bf16[64,512]{1,0:T(8,128)(2,1)S(1)} %get-tuple-element.20), channel_id=1, source_target_pairs={{0,2},{1,3},{2,0},{3,1},{4,6},{5,7},{6,4},{7,5},{8,10},{9,11},{10,... | collective-permute-start | bytes 196616 | tf_op jit(solution)/shard_map/ppermute | solution.py:31
  22.3 8.5 %collective-permute-start.11 = (bf16[64,512]{1,0:T(8,128)(2,1)S(1)}, bf16[64,512]{1,0:T(8,128)(2,1)S(1)}, u32[]{:S(2)}, u32[]{:S(2)}) collective-permute-start(bf16[64,512]{1,0:T(8,128)(2,1)S(1)} %get-tuple-element.21), channel_id=1, source_target_pairs={{0,4},{1,5},{2,6},{3,7},{4,0},{5,1},{6,2},{7,3},{8,12},{9,13},{10,... | collective-permute-start | bytes 196616 | tf_op jit(solution)/shard_map/ppermute | solution.py:31
  26.7 6.1 %collective-permute-start.12 = (bf16[64,512]{1,0:T(8,128)(2,1)S(1)}, bf16[64,512]{1,0:T(8,128)(2,1)S(1)}, u32[]{:S(2)}, u32[]{:S(2)}) collective-permute-start(bf16[64,512]{1,0:T(8,128)(2,1)S(1)} %get-tuple-element.22), channel_id=1, source_target_pairs={{0,6},{1,7},{2,4},{3,5},{4,2},{5,3},{6,0},{7,1},{8,14},{9,15},{10,... | collective-permute-start | bytes 196616 | tf_op jit(solution)/shard_map/ppermute | solution.py:31
  32.7 0.9 %copy-start.5 = (bf16[64,2048]{1,0:T(8,128)(2,1)}, bf16[64,2048]{1,0:T(8,128)(2,1)S(1)}, u32[]{:S(2)}) copy-start(bf16[64,2048]{1,0:T(8,128)(2,1)S(1)} %constant_dynamic-update-slice_fusion) | copy-start | bytes 786436

commit v4 on v3

v4 whole, which is shorter than its diff:
```python
import jax
import jax.numpy as jnp
from jax import lax
from jax.experimental import pallas as pl
from jax.experimental.pallas import tpu as pltpu
from jax.sharding import PartitionSpec as P

ITERS = 3
decay = 0.9
epsilon = 1e-06
F32 = jnp.float32
BF16 = jnp.bfloat16
ANY = pl.BlockSpec(memory_space=pl.ANY)
VMEM = pl.BlockSpec(memory_space=pltpu.VMEM)
SMEM = pl.BlockSpec(memory_space=pltpu.SMEM)


def place():
    position = lax.axis_index("bcol")
    return position >> 1, position & 1


def chip_pairs(step):
    return [(i, i ^ (step << 1)) for i in range(lax.axis_size("bcol"))]


def core_pairs():
    return [(i, i ^ 1) for i in range(lax.axis_size("bcol"))]


def permute(value, pairs):
    return lax.ppermute(value, "bcol", pairs)


def dot(left_side, right_side, contract=((1,), (0,))):
    return lax.dot_general(left_side, right_side, (contract, ((), ())), preferred_element_type=F32)


def call(kernel, out_shape, scratch, cost, ins=None, outs=None):
    flops, moved = cost

    def run(*operands):
        return pl.pallas_call(
            kernel,
            out_shape=out_shape,
            in_specs=ins or [VMEM] * len(operands),
            out_specs=outs or jax.tree.map(lambda _: VMEM, out_shape),
            scratch_shapes=scratch,
            compiler_params=pltpu.CompilerParams(vmem_limit_bytes=16 << 20),
            cost_estimate=pl.CostEstimate(flops=flops, bytes_accessed=moved, transcendentals=0),
        )(*operands)

    return run


def cut(chips, order, gradient, *refs):
    pieces, arrived = refs[:chips], refs[chips]
    column, _ = place()
    copies = []
    for step in sending(chips):
        start = pl.multiple_of((column ^ step) * order, order)
        copies.append(pltpu.make_async_copy(gradient.at[:, pl.ds(start, order)], pieces[step], arrived.at[step]))
    for copy in copies:
        copy.start()
    for copy in copies:
        copy.wait()


def sending(chips):
    return arrival(chips) + [0]


def deliver(chips, order, *refs):
    refresh, left_root, right_root, mine, taken = refs[:5]
    pieces, refs = refs[5 : 5 + chips], refs[5 + chips :]
    update, left_out, right_out, done = refs
    column, half = place()
    copies = []
    for step in range(chips):
        start = pl.multiple_of((column ^ step) * order, order)
        copies.append(pltpu.make_async_copy(pieces[step], update.at[:, pl.ds(start, order)], done.at[2 + step]))
    for copy in copies:
        copy.start()
    listed = refresh[0, 0] == column
    for entry in range(1, refresh.shape[1]):
        listed = jnp.logical_or(listed, refresh[0, entry] == column)
    first = jnp.logical_and(listed, half == 0)
    second = jnp.logical_and(listed, half == 1)

    def put(left, right):
        pltpu.make_async_copy(left, left_out, done.at[0]).start()
        pltpu.make_async_copy(right, right_out, done.at[1]).start()

    @pl.when(first)
    def _():
        put(mine, taken)

    @pl.when(second)
    def _():
        put(taken, mine)

    @pl.when(jnp.logical_not(listed))
    def _():
        put(left_root, right_root)

    pltpu.make_async_copy(mine, left_out, done.at[0]).wait()
    pltpu.make_async_copy(mine, right_out, done.at[1]).wait()
    for copy in copies:
        copy.wait()


def spans(chips):
    last = arrival(chips)[-2:]
    first = [(step, 0) for step in range(chips)] + [(step, 1) for step in range(chips) if step not in last]
    return first, [(step, 1) for step in last]


def row_of(piece, column, half, rows):
    step, other = piece
    return pl.ds(pl.multiple_of(((column ^ step) * 2 + (half ^ other)) * rows, rows), rows)


def prepare(chips, rows, order, left_mine, left_other, right_mine, right_other, old_left, old_right, old_other,
            left_first, left_last, right_full, left_kept, right_kept, other_kept, left_full, first_rows, last_rows,
            first_turned, last_turned):
    column, half = place()
    span = order // 2
    mine = pl.ds(pl.multiple_of(half * span, span), span)
    other = pl.ds(pl.multiple_of((1 - half) * span, span), span)
    left_full[mine, :] = left_mine[...]
    left_full[other, :] = left_other[...]
    right_full[mine, :] = right_mine[...]
    right_full[other, :] = right_other[...]
    groups = zip(spans(chips), (first_rows, last_rows), (first_turned, last_turned), (left_first, left_last))
    for pieces, gathered, turned, target in groups:
        for place_in, piece in enumerate(pieces):
            gathered[place_in * rows : (place_in + 1) * rows, :] = left_full[row_of(piece, column, half, rows), :]
        turned[...] = jnp.transpose(gathered[...])
        for step in range(chips):
            target[step * rows : (step + 1) * rows, :] = turned[row_of((step, 0), column, half, rows), :]
    left_kept[...] = decay * old_left[...]
    right_kept[...] = decay * old_right[...]
    other_kept[...] = decay * old_other[...].astype(F32)


def start_update(pieces, *refs):
    parts, (left_first, right_full, partial, block) = refs[: len(pieces)], refs[len(pieces) :]
    rows = parts[0].shape[0]
    for place_in, part in enumerate(parts):
        block[place_in * rows : (place_in + 1) * rows, :] = part[...]
    mixed = dot(block[...], right_full[...]).astype(BF16)
    partial[...] = dot(left_first[...], mixed)


def finish_update(pieces, chips, *refs):
    parts, refs = refs[: len(pieces)], refs[len(pieces) :]
    left_last, right_full, partial = refs[:3]
    updates, block = refs[3 : 3 + chips], refs[3 + chips]
    rows = parts[0].shape[0]
    for place_in, part in enumerate(parts):
        block[place_in * rows : (place_in + 1) * rows, :] = part[...]
    mixed = dot(block[...], right_full[...]).astype(BF16)
    result = (partial[...] + dot(left_last[...], mixed)).astype(BF16)
    for step in range(chips):
        updates[step][...] = result[step * rows : (step + 1) * rows, :]


def powers(moment):
    narrow = moment.astype(BF16)
    square = dot(narrow, narrow)
    return square, dot(square.astype(BF16), narrow), narrow


def refreshed(order, chips, *refs):
    parts, refs = refs[: 2 * chips], refs[2 * chips :]
    refreshed_body(order, parts, *refs)


def refreshed_body(order, parts, left_kept, right_kept, other_kept, left_out, right_out, root_mine, root_other,
                   whole, new_left, new_right, stat, root, done):
    column, half = place()
    chips, rows = len(parts) // 2, parts[0].shape[0]
    for which, part in enumerate(parts):
        whole[row_of((which % chips, which // chips), column, half, rows), :] = part[...]
    span = order // 2
    mine = pl.ds(pl.multiple_of(half * span, span), span)
    other = pl.ds(pl.multiple_of((1 - half) * span, span), span)
    rate = 1.0 - decay
    full = whole[...]
    new_left[...] = left_kept[...] + rate * dot(whole[mine, :], full, ((1,), (1,)))
    left_copy = pltpu.make_async_copy(new_left, left_out, done.at[0])
    left_copy.start()
    new_right[...] = right_kept[...] + rate * dot(whole[:, mine], full, ((0,), (0,)))
    right_copy = pltpu.make_async_copy(new_right, right_out, done.at[1])
    right_copy.start()

    @pl.when(half == 0)
    def _():
        stat[mine, :] = new_left[...]
        stat[other, :] = other_kept[...] + rate * dot(whole[other, :], full, ((1,), (1,)))

    @pl.when(half == 1)
    def _():
        stat[mine, :] = new_right[...]
        stat[other, :] = other_kept[...] + rate * dot(whole[:, other], full, ((0,), (0,)))

    shape = (order, order)
    diagonal = lax.broadcasted_iota(jnp.int32, shape, 0) == lax.broadcasted_iota(jnp.int32, shape, 1)
    shifted = stat[...] + jnp.where(diagonal, epsilon, 0.0)
    total = jnp.sum(jnp.sum(shifted * shifted, axis=1, keepdims=True), axis=0, keepdims=True)
    scaling = 2.5 / jnp.sqrt(total)
    moment = scaling * shifted
    first = moment
    for _ in range(ITERS - 2):
        square, cube, narrow = powers(moment)
        small = (20.0 / -256.0) * moment + (1.0 / 256.0) * square
        moment = (
            (625.0 / 256.0) * moment
            - (500.0 / 256.0) * square
            + (150.0 / 256.0) * cube
            + dot(cube.astype(BF16), small.astype(BF16))
        )
    square, cube, narrow = powers(moment)
    small = (250.0 / 4096.0) * moment - (25.0 / 4096.0) * square + (1.0 / 4096.0) * cube
    rest = (
        (-0.3125 - 3125.0 / 4096.0) * moment
        + (3125.0 / 4096.0) * square
        - (1250.0 / 4096.0) * cube
        + dot(cube.astype(BF16), small.astype(BF16))
    )
    product = dot(rest.astype(BF16), first.astype(BF16))
    result = 1.25 * rest - (0.25 * 1.5625) * first - 0.25 * product + jnp.where(diagonal, 1.25 * 1.5625, 0.0)
    root[...] = (jnp.sqrt(jnp.sqrt(scaling)) * result).astype(BF16)
    root_mine[...] = root[mine, :]
    root_other[...] = root[other, :]
    left_copy.wait()
    right_copy.wait()


def step(gradient, left_stats, right_stats, left_roots, right_roots, refresh):
    _, half = place()
    chips = lax.axis_size("bcol") // 2
    rows = gradient.shape[0]
    order = left_stats.shape[2]
    span = order // 2
    is_second = half == 1
    left_old, right_old = left_stats[0], right_stats[0]
    left_root, right_root = left_roots[0], right_roots[0]

    def shape(r, c, t):
        return jax.ShapeDtypeStruct((r, c), t)

    def kernel(f, *static):
        return lambda *refs: f(*static, *refs)

    def signals(count):
        return pltpu.SemaphoreType.DMA((count,))

    pieces = call(
        kernel(cut, chips, order), [shape(rows, order, BF16)] * chips, [signals(chips)], (0, rows * chips * order * 4),
        [ANY],
    )(gradient)
    mine = [pieces[0]] + [permute(pieces[step], chip_pairs(step)) for step in range(1, chips)]
    given_stat = jnp.where(is_second, left_old, right_old).astype(BF16)
    left_other, right_other, old_other = [permute(x, core_pairs()) for x in (left_root, right_root, given_stat)]
    other = [permute(x, core_pairs()) for x in mine]

    first, last = spans(chips)
    wide = [len(pieces) * rows for pieces in (first, last)]
    left_first, left_last, right_full, left_kept, right_kept, other_kept = call(
        kernel(prepare, chips, rows, order),
        (shape(span, wide[0], BF16), shape(span, wide[1], BF16), shape(order, order, BF16), *[shape(span, order, F32)] * 3),
        [pltpu.VMEM((order, order), BF16)]
        + [pltpu.VMEM((width, order), BF16) for width in wide]
        + [pltpu.VMEM((order, width), BF16) for width in wide],
        (0, 4 * order * order * 2),
    )(left_root, left_other, right_root, right_other, left_old, right_old, old_other)
    held = (mine, other)
    partial = call(
        kernel(start_update, first),
        shape(span, order, F32),
        [pltpu.VMEM((wide[0], order), BF16)],
        (3 * wide[0] * order**2, 4 * order * order * 2),
    )(*[held[side][step] for step, side in first], left_first, right_full)
    updates = call(
        kernel(finish_update, last, chips),
        [shape(rows, order, BF16)] * chips,
        [pltpu.VMEM((wide[1], order), BF16)],
        (3 * wide[1] * order**2, 4 * order * order * 2),
    )(*[held[side][step] for step, side in last], left_last, right_full, partial)
    returned = [updates[0]] + [permute(updates[step], chip_pairs(step)) for step in range(1, chips)]
    left_new, right_new, root_mine, root_other = call(
        kernel(refreshed, order, chips),
        (shape(span, order, F32), shape(span, order, F32), shape(span, order, BF16), shape(span, order, BF16)),
        [
            pltpu.VMEM((order, order), BF16),
            pltpu.VMEM((span, order), F32),
            pltpu.VMEM((span, order), F32),
            pltpu.VMEM((order, order), F32),
            pltpu.VMEM((order, order), BF16),
            signals(2),
        ],
        (20 * order**3, 8 * order * order * 4),
        None,
        (ANY, ANY, VMEM, VMEM),
    )(*mine, *other, left_kept, right_kept, other_kept)
    taken = permute(root_other, core_pairs())
    update, left_out, right_out = call(
        kernel(deliver, chips, order),
        (shape(rows, chips * order, BF16), shape(span, order, BF16), shape(span, order, BF16)),
        [signals(2 + chips)],
        (0, 4 * rows * chips * order * 4),
        [SMEM] + [VMEM] * (4 + chips),
        (ANY, ANY, ANY),
    )(refresh, left_root, right_root, root_mine, taken, *returned)
    return (update, left_new[None], right_new[None], left_out[None], right_out[None])


def arrival(chips):
    return list(range(chips // 2, chips)) + list(range(1, chips // 2))


def solution(mesh):
    block = P("brow", "bcol", None)
    rows = P(("brow", "bcol"), None)
    in_specs = (rows, block, block, block, block, P("brow", None))
    out_specs = (rows, block, block, block, block)
    return jax.shard_map(step, mesh=mesh, in_specs=in_specs, out_specs=out_specs, check_vma=False)
```

time: 33.8 us -> 36.2 us (1.071)
  waiting for transfers between devices: 8.59 us -> 10.7 us
  Pallas kernels: 4.83 us -> 6.18 us
  starting transfers between devices: 16.4 us -> 15.4 us
  other arithmetic: 2.25 us -> 1.37 us
  local copies, waits for them, and re-layouts: 0.11 us -> 0.97 us
    ppermute x14, waiting for transfers between devices: 8.59 us -> 10.7 us  [permute(): return lax.ppermute(value, 'bcol', pairs)]
    pallas_call x3 -> x6, Pallas kernels: 4.83 us -> 6.18 us  [run(): pl.pallas_call(kernel, out_shape=out_shape, in_specs=ins or [VMEM] * len(...]
    unnamed x12 -> x10, local copies, waits for them, and re-layouts: 0.03 us -> 0.97 us
    ppermute x14, starting transfers between devices: 16.4 us -> 15.4 us  [permute(): return lax.ppermute(value, 'bcol', pairs)]
    broadcast_in_dim x1 -> x0, other arithmetic: 0.85 us -> none  [step(): right_out[None]]
  transfers between devices with their start and end apart: 14 -> 14, of which waited for: 5 -> 7; matrix products, arithmetic and copies ran while one was open for 0% -> 4% of each run, Pallas kernels for 0% -> 4%
where the time goes in v4:
time: 36.2 us; the launch traced here: 36.1 us
  starting transfers between devices  15.4 us (43%)
  waiting for transfers between devices  10.7 us (30%)
  Pallas kernels  6.18 us (17%)
  between operations  1.39 us (4%)
  other arithmetic  1.37 us (4%)
  local copies, waits for them, and re-layouts  0.97 us (3%)
    ppermute x14, starting transfers between devices, permute(): return lax.ppermute(value, 'bcol', pairs)  15.4 us
    ppermute x14, waiting for transfers between devices, permute(): return lax.ppermute(value, 'bcol', pairs)  10.7 us
    pallas_call x6, Pallas kernels, run(): pl.pallas_call(kernel, out_shape=out_shape, in_specs=ins or [VMEM] * len(...  6.18 us
    convert_element_type x1, other arithmetic, step(): given_stat = jnp.where(is_second, left_old, right_old).astype(BF16)  1.37 us
    unnamed x10, local copies, waits for them, and re-layouts  0.97 us
  transfers between devices with their start and end apart: 14, of which 7 were waited for; matrix products, arithmetic and copies ran while one was open for 4% of the time, Pallas kernels for 4%

profile of v4, /device:TPU:0, one launch (start us, length us, event | category | flops | bytes accessed | tf_op | source)
XLA Modules:
  0.0 36.1 jit_solution(15182636899966186017)
XLA Ops:
  0.6 0.6 %collective-permute-start.7 = (bf16[256,512]{1,0:T(8,128)(2,1)}, bf16[256,512]{1,0:T(8,128)(2,1)S(1)}, u32[]{:S(2)}, u32[]{:S(2)}) collective-permute-start(bf16[256,512]{1,0:T(8,128)(2,1)} %bitcast.12), channel_id=1, source_target_pairs={{0,1},{1,0},{2,3},{3,2},{4,5},{5,4},{6,7},{7,6},{8,9},{9,8},{10,11... | collective-permute-start | bytes 786440 | tf_op jit(solution)/shard_map/ppermute | solution.py:32
  1.2 0.1 collective-permute-start.8
  1.3 1.4 %select_convert_fusion = bf16[256,512]{1,0:T(8,128)(2,1)S(1)} fusion(pred[]{:T(512)S(6)} %eq.3, f32[1,256,512]{2,1,0:T(8,128)} %param.8, f32[1,256,512]{2,1,0:T(8,128)} %param.7), kind=kLoop, calls=%fused_computation | loop fusion | flops 131072 | bytes 1310721 | tf_op jit(solution)/shard_map/convert_element_type | solution.py:264
  2.7 0.0 copy-start.2
  2.7 0.5 %collective-permute-start.9 = (bf16[256,512]{1,0:T(8,128)(2,1)S(1)}, bf16[256,512]{1,0:T(8,128)(2,1)S(1)}, u32[]{:S(2)}, u32[]{:S(2)}) collective-permute-start(bf16[256,512]{1,0:T(8,128)(2,1)S(1)} %select_convert_fusion), channel_id=1, source_target_pairs={{0,1},{1,0},{2,3},{3,2},{4,5},{5,4},{6,7},{7,6},{8,9},{9,8},{10,11... | collective-permute-start | bytes 786440 | tf_op jit(solution)/shard_map/ppermute | solution.py:32
  3.2 0.9 %copy-done.4 = bf16[64,2048]{1,0:T(8,128)(2,1)S(1)} copy-done((bf16[64,2048]{1,0:T(8,128)(2,1)S(1)}, bf16[64,2048]{1,0:T(8,128)(2,1)}, u32[]{:S(2)}) %copy-start.4) | copy-done | bytes 262168
  4.1 0.1 shard_map.101
  4.2 3.7 %collective-permute-start.1 = (bf16[64,512]{1,0:T(8,128)(2,1)S(1)}, bf16[64,512]{1,0:T(8,128)(2,1)S(1)}, u32[]{:S(2)}, u32[]{:S(2)}) collective-permute-start(bf16[64,512]{1,0:T(8,128)(2,1)S(1)} %get-tuple-element.28), channel_id=1, source_target_pairs={{0,4},{1,5},{2,6},{3,7},{4,0},{5,1},{6,2},{7,3},{8,12},{9,13},{10,... | collective-permute-start | bytes 196616 | tf_op jit(solution)/shard_map/ppermute | solution.py:32
  7.9 1.6 %collective-permute-start = (bf16[64,512]{1,0:T(8,128)(2,1)S(1)}, bf16[64,512]{1,0:T(8,128)(2,1)S(1)}, u32[]{:S(2)}, u32[]{:S(2)}) collective-permute-start(bf16[64,512]{1,0:T(8,128)(2,1)S(1)} %get-tuple-element.27), channel_id=1, source_target_pairs={{0,2},{1,3},{2,0},{3,1},{4,6},{5,7},{6,4},{7,5},{8,10},{9,11},{10,... | collective-permute-start | bytes 196616 | tf_op jit(solution)/shard_map/ppermute | solution.py:32
  9.5 2.3 %collective-permute-done.1.refs_2_ = bf16[64,512]{1,0:T(8,128)(2,1)S(1)} collective-permute-done((bf16[64,512]{1,0:T(8,128)(2,1)S(1)}, bf16[64,512]{1,0:T(8,128)(2,1)S(1)}, u32[]{:S(2)}, u32[]{:S(2)}) %collective-permute-start.1) | collective-permute-done | bytes 65568 | tf_op jit(solution)/shard_map/ppermute | solution.py:32
  11.8 3.7 %collective-permute-start.2 = (bf16[64,512]{1,0:T(8,128)(2,1)S(1)}, bf16[64,512]{1,0:T(8,128)(2,1)S(1)}, u32[]{:S(2)}, u32[]{:S(2)}) collective-permute-start(bf16[64,512]{1,0:T(8,128)(2,1)S(1)} %get-tuple-element.29), channel_id=1, source_target_pairs={{0,6},{1,7},{2,4},{3,5},{4,2},{5,3},{6,0},{7,1},{8,14},{9,15},{10,... | collective-permute-start | bytes 196616 | tf_op jit(solution)/shard_map/ppermute | solution.py:32
  15.6 0.0 collective-permute-done.refs_1_
  15.6 0.0 collective-permute-start.3
  15.6 2.3 %collective-permute-done.2.refs_3_ = bf16[64,512]{1,0:T(8,128)(2,1)S(1)} collective-permute-done((bf16[64,512]{1,0:T(8,128)(2,1)S(1)}, bf16[64,512]{1,0:T(8,128)(2,1)S(1)}, u32[]{:S(2)}, u32[]{:S(2)}) %collective-permute-start.2) | collective-permute-done | bytes 65568 | tf_op jit(solution)/shard_map/ppermute | solution.py:32
  17.9 0.0 collective-permute-start.5
  17.9 0.0 collective-permute-done.7.refs_1_
  17.9 0.5 %collective-permute-start.4 = (bf16[64,512]{1,0:T(8,128)(2,1)S(1)}, bf16[64,512]{1,0:T(8,128)(2,1)S(1)}, u32[]{:S(2)}, u32[]{:S(2)}) collective-permute-start(bf16[64,512]{1,0:T(8,128)(2,1)S(1)} %collective-permute-done.refs_1_), channel_id=1, source_target_pairs={{0,1},{1,0},{2,3},{3,2},{4,5},{5,4},{6,7},{7,6},{8,9},{9,8},{10,11... | collective-permute-start | bytes 196616 | tf_op jit(solution)/shard_map/ppermute | solution.py:32
  18.4 0.1 collective-permute-start.6
  18.5 0.4 %shard_map.102 = (bf16[256,384]{1,0:T(8,128)(2,1)S(1)}, bf16[256,128]{1,0:T(8,128)(2,1)S(1)}, bf16[512,512]{1,0:T(8,128)(2,1)S(1)}, f32[256,512]{1,0:T(8,128)S(1...) custom-call(bf16[256,512]{1,0:T(8,128)(2,1)S(1)} %bitcast.13, bf16[256,512]{1,0:T(8,128)(2,1)S(1)} %collective-permute-done.7.refs_1_, ...), custom_call_target="tpu_custom_call" | custom-call | bytes 2097152 | tf_op jit(solution)/shard_map/pallas_call | solution.py:43
  18.9 0.3 collective-permute-done.5.refs_6_.refs_5_
  19.1 0.2 collective-permute-done.4.refs_5_.refs_1_
  19.3 0.4 collective-permute-done.6.refs_7_.refs_0_
  19.7 3.8 %shard_map.103 = (f32[256,512]{1,0:T(8,128)}, f32[256,512]{1,0:T(8,128)}, bf16[256,512]{1,0:T(8,128)(2,1)S(1)}, bf16[256,512]{1,0:T(8,128)(2,1)S(1)}) custom-call(bf16[64,512]{1,0:T(8,128)(2,1)S(1)} %get-tuple-element.26.refs_0_, bf16[64,512]{1,0:T(8,128)(2,1)S(1)} %collective-permute-done.refs_1_, bf16[64,512]{1,0:T(8,128)(2,1)S(1)} %collective-permute-done.1.refs_2_, ...), custom_call_target="tpu_custom_call" | custom-call | flops 2684354560 | bytes 8388608 | tf_op jit(solution)/shard_map/pallas_call | solution.py:43
  23.4 0.2 collective-permute-start.10
  23.7 0.6 %shard_map.104.refs_4_ = f32[256,512]{1,0:T(8,128)S(1)} custom-call(bf16[64,512]{1,0:T(8,128)(2,1)S(1)} %get-tuple-element.26.refs_0_, bf16[64,512]{1,0:T(8,128)(2,1)S(1)} %collective-permute-done.refs_1_, bf16[64,512]{1,0:T(8,128)(2,1)S(1)} %collective-permute-done.1.refs_2_, bf16[64,512]{1,0:T(8,128)(2,1)S(1)} %collective-permute-done.2.refs_3_, ...), custom_call_target="tpu_custom_call" | custom-call | flops 301989888 | bytes 2097152 | tf_op jit(solution)/shard_map/pallas_call | solution.py:43
  24.3 0.4 %shard_map.105 = (bf16[64,512]{1,0:T(8,128)(2,1)S(1)}, bf16[64,512]{1,0:T(8,128)(2,1)S(1)}, bf16[64,512]{1,0:T(8,128)(2,1)S(1)}, bf16[64,512]{1,0:T(8,128)(2,1)S(1)}) custom-call(bf16[64,512]{1,0:T(8,128)(2,1)S(1)} %collective-permute-done.6.refs_7_.refs_0_, bf16[64,512]{1,0:T(8,128)(2,1)S(1)} %collective-permute-done.4.refs_5_.refs_1_, ...), custom_call_target="tpu_custom_call" | custom-call | flops 100663296 | bytes 2097152 | tf_op jit(solution)/shard_map/pallas_call | solution.py:43
  24.7 0.1 collective-permute-start.11
  24.8 4.3 %collective-permute-start.12 = (bf16[64,512]{1,0:T(8,128)(2,1)S(1)}, bf16[64,512]{1,0:T(8,128)(2,1)S(1)}, u32[]{:S(2)}, u32[]{:S(2)}) collective-permute-start(bf16[64,512]{1,0:T(8,128)(2,1)S(1)} %get-tuple-element.40), channel_id=1, source_target_pairs={{0,4},{1,5},{2,6},{3,7},{4,0},{5,1},{6,2},{7,3},{8,12},{9,13},{10,... | collective-permute-start | bytes 196616 | tf_op jit(solution)/shard_map/ppermute | solution.py:32
  29.1 0.1 collective-permute-start.13
  29.8 3.3 %collective-permute-done.12.refs_7_ = bf16[64,512]{1,0:T(8,128)(2,1)S(1)} collective-permute-done((bf16[64,512]{1,0:T(8,128)(2,1)S(1)}, bf16[64,512]{1,0:T(8,128)(2,1)S(1)}, u32[]{:S(2)}, u32[]{:S(2)}) %collective-permute-start.12) | collective-permute-done | bytes 65568 | tf_op jit(solution)/shard_map/ppermute | solution.py:32
  33.2 2.0 %collective-permute-done.13.refs_8_ = bf16[64,512]{1,0:T(8,128)(2,1)S(1)} collective-permute-done((bf16[64,512]{1,0:T(8,128)(2,1)S(1)}, bf16[64,512]{1,0:T(8,128)(2,1)S(1)}, u32[]{:S(2)}, u32[]{:S(2)}) %collective-permute-start.13) | collective-permute-done | bytes 65568 | tf_op jit(solution)/shard_map/ppermute | solution.py:32
  35.1 0.9 %shard_map.106 = (bf16[64,2048]{1,0:T(8,128)(2,1)}, bf16[256,512]{1,0:T(8,128)(2,1)}, bf16[256,512]{1,0:T(8,128)(2,1)}) custom-call(s32[1,1]{1,0:T(1,128)S(6)} %copy.11.refs_0_, bf16[256,512]{1,0:T(8,128)(2,1)S(1)} %bitcast.14, bf16[256,512]{1,0:T(8,128)(2,1)S(1)} %bitcast.17, bf16[256,512]{1,0:T(8,128)(2,1)S(1)} %get-tuple-element.33.refs_3_, ...), custom_call_target="tpu_custom_call" | custom-call | bytes 2097152 | tf_op jit(solution)/shard_map/pallas_call | solution.py:43
  (13 shorter events, 0.0 us)
Async XLA Ops:
  0.6 17.3 %collective-permute-start.7 = (bf16[256,512]{1,0:T(8,128)(2,1)}, bf16[256,512]{1,0:T(8,128)(2,1)S(1)}, u32[]{:S(2)}, u32[]{:S(2)}) collective-permute-start(bf16[256,512]{1,0:T(8,128)(2,1)} %bitcast.12), channel_id=1, source_target_pairs={{0,1},{1,0},{2,3},{3,2},{4,5},{5,4},{6,7},{7,6},{8,9},{9,8},{10,11... | collective-permute-start | bytes 786440 | tf_op jit(solution)/shard_map/ppermute | solution.py:32
  1.2 17.2 %collective-permute-start.8 = (bf16[256,512]{1,0:T(8,128)(2,1)}, bf16[256,512]{1,0:T(8,128)(2,1)S(1)}, u32[]{:S(2)}, u32[]{:S(2)}) collective-permute-start(bf16[256,512]{1,0:T(8,128)(2,1)} %bitcast.15), channel_id=1, source_target_pairs={{0,1},{1,0},{2,3},{3,2},{4,5},{5,4},{6,7},{7,6},{8,9},{9,8},{10,11... | collective-permute-start | bytes 786440 | tf_op jit(solution)/shard_map/ppermute | solution.py:32
  1.3 17.2 %copy-start = (f32[1,256,512]{2,1,0:T(8,128)S(1)}, f32[1,256,512]{2,1,0:T(8,128)}, u32[]{:S(2)}) copy-start(f32[1,256,512]{2,1,0:T(8,128)} %param.7) | copy-start | bytes 1572868
  1.3 17.2 %copy-start.1 = (f32[1,256,512]{2,1,0:T(8,128)S(1)}, f32[1,256,512]{2,1,0:T(8,128)}, u32[]{:S(2)}) copy-start(f32[1,256,512]{2,1,0:T(8,128)} %param.8) | copy-start | bytes 1572868
  1.3 17.2 %copy-start.3 = (bf16[1,256,512]{2,1,0:T(8,128)(2,1)S(1)}, bf16[1,256,512]{2,1,0:T(8,128)(2,1)}, u32[]{:S(2)}) copy-start(bf16[1,256,512]{2,1,0:T(8,128)(2,1)} %param.10) | copy-start | bytes 786436
  2.7 15.8 %copy-start.2 = (bf16[1,256,512]{2,1,0:T(8,128)(2,1)S(1)}, bf16[1,256,512]{2,1,0:T(8,128)(2,1)}, u32[]{:S(2)}) copy-start(bf16[1,256,512]{2,1,0:T(8,128)(2,1)} %param.9) | copy-start | bytes 786436
  2.7 15.8 %collective-permute-start.9 = (bf16[256,512]{1,0:T(8,128)(2,1)S(1)}, bf16[256,512]{1,0:T(8,128)(2,1)S(1)}, u32[]{:S(2)}, u32[]{:S(2)}) collective-permute-start(bf16[256,512]{1,0:T(8,128)(2,1)S(1)} %select_convert_fusion), channel_id=1, source_target_pairs={{0,1},{1,0},{2,3},{3,2},{4,5},{5,4},{6,7},{7,6},{8,9},{9,8},{10,11... | collective-permute-start | bytes 786440 | tf_op jit(solution)/shard_map/ppermute | solution.py:32
  3.2 0.9 %copy-start.4 = (bf16[64,2048]{1,0:T(8,128)(2,1)S(1)}, bf16[64,2048]{1,0:T(8,128)(2,1)}, u32[]{:S(2)}) copy-start(bf16[64,2048]{1,0:T(8,128)(2,1)} %refs_0_.2) | copy-start | bytes 786436
  4.2 7.6 %collective-permute-start.1 = (bf16[64,512]{1,0:T(8,128)(2,1)S(1)}, bf16[64,512]{1,0:T(8,128)(2,1)S(1)}, u32[]{:S(2)}, u32[]{:S(2)}) collective-permute-start(bf16[64,512]{1,0:T(8,128)(2,1)S(1)} %get-tuple-element.28), channel_id=1, source_target_pairs={{0,4},{1,5},{2,6},{3,7},{4,0},{5,1},{6,2},{7,3},{8,12},{9,13},{10,... | collective-permute-start | bytes 196616 | tf_op jit(solution)/shard_map/ppermute | solution.py:32
  7.9 7.6 %collective-permute-start = (bf16[64,512]{1,0:T(8,128)(2,1)S(1)}, bf16[64,512]{1,0:T(8,128)(2,1)S(1)}, u32[]{:S(2)}, u32[]{:S(2)}) collective-permute-start(bf16[64,512]{1,0:T(8,128)(2,1)S(1)} %get-tuple-element.27), channel_id=1, source_target_pairs={{0,2},{1,3},{2,0},{3,1},{4,6},{5,7},{6,4},{7,5},{8,10},{9,11},{10,... | collective-permute-start | bytes 196616 | tf_op jit(solution)/shard_map/ppermute | solution.py:32
  11.8 6.1 %collective-permute-start.2 = (bf16[64,512]{1,0:T(8,128)(2,1)S(1)}, bf16[64,512]{1,0:T(8,128)(2,1)S(1)}, u32[]{:S(2)}, u32[]{:S(2)}) collective-permute-start(bf16[64,512]{1,0:T(8,128)(2,1)S(1)} %get-tuple-element.29), channel_id=1, source_target_pairs={{0,6},{1,7},{2,4},{3,5},{4,2},{5,3},{6,0},{7,1},{8,14},{9,15},{10,... | collective-permute-start | bytes 196616 | tf_op jit(solution)/shard_map/ppermute | solution.py:32
  15.6 3.3 %collective-permute-start.3 = (bf16[64,512]{1,0:T(8,128)(2,1)S(1)}, bf16[64,512]{1,0:T(8,128)(2,1)S(1)}, u32[]{:S(2)}, u32[]{:S(2)}) collective-permute-start(bf16[64,512]{1,0:T(8,128)(2,1)S(1)} %get-tuple-element.26.refs_0_), channel_id=1, source_target_pairs={{0,1},{1,0},{2,3},{3,2},{4,5},{5,4},{6,7},{7,6},{8,9},{9,8},{10,11... | collective-permute-start | bytes 196616 | tf_op jit(solution)/shard_map/ppermute | solution.py:32
  17.9 1.3 %collective-permute-start.5 = (bf16[64,512]{1,0:T(8,128)(2,1)S(1)}, bf16[64,512]{1,0:T(8,128)(2,1)S(1)}, u32[]{:S(2)}, u32[]{:S(2)}) collective-permute-start(bf16[64,512]{1,0:T(8,128)(2,1)S(1)} %collective-permute-done.1.refs_2_), channel_id=1, source_target_pairs={{0,1},{1,0},{2,3},{3,2},{4,5},{5,4},{6,7},{7,6},{8,9},{9,8},{10,11... | collective-permute-start | bytes 196616 | tf_op jit(solution)/shard_map/ppermute | solution.py:32
  17.9 1.4 %collective-permute-start.4 = (bf16[64,512]{1,0:T(8,128)(2,1)S(1)}, bf16[64,512]{1,0:T(8,128)(2,1)S(1)}, u32[]{:S(2)}, u32[]{:S(2)}) collective-permute-start(bf16[64,512]{1,0:T(8,128)(2,1)S(1)} %collective-permute-done.refs_1_), channel_id=1, source_target_pairs={{0,1},{1,0},{2,3},{3,2},{4,5},{5,4},{6,7},{7,6},{8,9},{9,8},{10,11... | collective-permute-start | bytes 196616 | tf_op jit(solution)/shard_map/ppermute | solution.py:32
  18.4 1.3 %collective-permute-start.6 = (bf16[64,512]{1,0:T(8,128)(2,1)S(1)}, bf16[64,512]{1,0:T(8,128)(2,1)S(1)}, u32[]{:S(2)}, u32[]{:S(2)}) collective-permute-start(bf16[64,512]{1,0:T(8,128)(2,1)S(1)} %collective-permute-done.2.refs_3_), channel_id=1, source_target_pairs={{0,1},{1,0},{2,3},{3,2},{4,5},{5,4},{6,7},{7,6},{8,9},{9,8},{10,11... | collective-permute-start | bytes 196616 | tf_op jit(solution)/shard_map/ppermute | solution.py:32
  23.4 11.7 %collective-permute-start.10 = (bf16[256,512]{1,0:T(8,128)(2,1)S(1)}, bf16[256,512]{1,0:T(8,128)(2,1)S(1)}, u32[]{:S(2)}, u32[]{:S(2)}) collective-permute-start(bf16[256,512]{1,0:T(8,128)(2,1)S(1)} %get-tuple-element.34), channel_id=1, source_target_pairs={{0,1},{1,0},{2,3},{3,2},{4,5},{5,4},{6,7},{7,6},{8,9},{9,8},{10,11... | collective-permute-start | bytes 786440 | tf_op jit(solution)/shard_map/ppermute | solution.py:32
  24.7 5.1 %collective-permute-start.11 = (bf16[64,512]{1,0:T(8,128)(2,1)S(1)}, bf16[64,512]{1,0:T(8,128)(2,1)S(1)}, u32[]{:S(2)}, u32[]{:S(2)}) collective-permute-start(bf16[64,512]{1,0:T(8,128)(2,1)S(1)} %get-tuple-element.39), channel_id=1, source_target_pairs={{0,2},{1,3},{2,0},{3,1},{4,6},{5,7},{6,4},{7,5},{8,10},{9,11},{10,... | collective-permute-start | bytes 196616 | tf_op jit(solution)/shard_map/ppermute | solution.py:32
  24.8 8.4 %collective-permute-start.12 = (bf16[64,512]{1,0:T(8,128)(2,1)S(1)}, bf16[64,512]{1,0:T(8,128)(2,1)S(1)}, u32[]{:S(2)}, u32[]{:S(2)}) collective-permute-start(bf16[64,512]{1,0:T(8,128)(2,1)S(1)} %get-tuple-element.40), channel_id=1, source_target_pairs={{0,4},{1,5},{2,6},{3,7},{4,0},{5,1},{6,2},{7,3},{8,12},{9,13},{10,... | collective-permute-start | bytes 196616 | tf_op jit(solution)/shard_map/ppermute | solution.py:32
  29.1 6.1 %collective-permute-start.13 = (bf16[64,512]{1,0:T(8,128)(2,1)S(1)}, bf16[64,512]{1,0:T(8,128)(2,1)S(1)}, u32[]{:S(2)}, u32[]{:S(2)}) collective-permute-start(bf16[64,512]{1,0:T(8,128)(2,1)S(1)} %get-tuple-element.41), channel_id=1, source_target_pairs={{0,6},{1,7},{2,4},{3,5},{4,2},{5,3},{6,0},{7,1},{8,14},{9,15},{10,... | collective-permute-start | bytes 196616 | tf_op jit(solution)/shard_map/ppermute | solution.py:32

commit v5 on v4

--- a/solution.py
+++ b/solution.py
@@ -120,17 +120,18 @@
     return pl.ds(pl.multiple_of(((column ^ step) * 2 + (half ^ other)) * rows, rows), rows)
 
 
-def prepare(chips, rows, order, left_mine, left_other, right_mine, right_other, old_left, old_right, old_other,
-            left_first, left_last, right_full, left_kept, right_kept, other_kept, left_full, first_rows, last_rows,
-            first_turned, last_turned):
+def prepare(chips, rows, order, left_mine, right_mine, old_left, old_right, packed,
+            own_other, left_first, left_last, right_full, left_kept, right_kept, left_full, first_rows,
+            last_rows, first_turned, last_turned):
     column, half = place()
     span = order // 2
     mine = pl.ds(pl.multiple_of(half * span, span), span)
     other = pl.ds(pl.multiple_of((1 - half) * span, span), span)
     left_full[mine, :] = left_mine[...]
-    left_full[other, :] = left_other[...]
+    own_other[...] = packed[0:rows, :]
+    left_full[other, :] = packed[rows : rows + span, :]
     right_full[mine, :] = right_mine[...]
-    right_full[other, :] = right_other[...]
+    right_full[other, :] = packed[rows + span : rows + 2 * span, :]
     groups = zip(spans(chips), (first_rows, last_rows), (first_turned, last_turned), (left_first, left_last))
     for pieces, gathered, turned, target in groups:
         for place_in, piece in enumerate(pieces):
@@ -140,7 +141,6 @@
             target[step * rows : (step + 1) * rows, :] = turned[row_of((step, 0), column, half, rows), :]
     left_kept[...] = decay * old_left[...]
     right_kept[...] = decay * old_right[...]
-    other_kept[...] = decay * old_other[...].astype(F32)
 
 
 def start_update(pieces, *refs):
@@ -176,7 +176,7 @@
     refreshed_body(order, parts, *refs)
 
 
-def refreshed_body(order, parts, left_kept, right_kept, other_kept, left_out, right_out, root_mine, root_other,
+def refreshed_body(order, parts, left_kept, right_kept, old_other, left_out, right_out, root_mine, root_other,
                    whole, new_left, new_right, stat, root, done):
     column, half = place()
     chips, rows = len(parts) // 2, parts[0].shape[0]
@@ -197,12 +197,12 @@
     @pl.when(half == 0)
     def _():
         stat[mine, :] = new_left[...]
-        stat[other, :] = other_kept[...] + rate * dot(whole[other, :], full, ((1,), (1,)))
+        stat[other, :] = decay * old_other[...].astype(F32) + rate * dot(whole[other, :], full, ((1,), (1,)))
 
     @pl.when(half == 1)
     def _():
         stat[mine, :] = new_right[...]
-        stat[other, :] = other_kept[...] + rate * dot(whole[:, other], full, ((0,), (0,)))
+        stat[other, :] = decay * old_other[...].astype(F32) + rate * dot(whole[:, other], full, ((0,), (0,)))
 
     shape = (order, order)
     diagonal = lax.broadcasted_iota(jnp.int32, shape, 0) == lax.broadcasted_iota(jnp.int32, shape, 1)
@@ -243,7 +243,6 @@
     rows = gradient.shape[0]
     order = left_stats.shape[2]
     span = order // 2
-    is_second = half == 1
     left_old, right_old = left_stats[0], right_stats[0]
     left_root, right_root = left_roots[0], right_roots[0]
 
@@ -261,20 +260,21 @@
         [ANY],
     )(gradient)
     mine = [pieces[0]] + [permute(pieces[step], chip_pairs(step)) for step in range(1, chips)]
-    given_stat = jnp.where(is_second, left_old, right_old).astype(BF16)
-    left_other, right_other, old_other = [permute(x, core_pairs()) for x in (left_root, right_root, given_stat)]
-    other = [permute(x, core_pairs()) for x in mine]
-
+    given_stat = jnp.where(half == 1, left_old, right_old).astype(BF16)
+    packed = jnp.concatenate([pieces[0], left_root, right_root], 0)
+    packed = permute(packed, core_pairs())
+    old_other = permute(given_stat, core_pairs())
     first, last = spans(chips)
     wide = [len(pieces) * rows for pieces in (first, last)]
-    left_first, left_last, right_full, left_kept, right_kept, other_kept = call(
+    own_other, left_first, left_last, right_full, left_kept, right_kept = call(
         kernel(prepare, chips, rows, order),
-        (shape(span, wide[0], BF16), shape(span, wide[1], BF16), shape(order, order, BF16), *[shape(span, order, F32)] * 3),
+        (shape(rows, order, BF16), shape(span, wide[0], BF16), shape(span, wide[1], BF16), shape(order, order, BF16), *[shape(span, order, F32)] * 2),
         [pltpu.VMEM((order, order), BF16)]
         + [pltpu.VMEM((width, order), BF16) for width in wide]
         + [pltpu.VMEM((order, width), BF16) for width in wide],
         (0, 4 * order * order * 2),
-    )(left_root, left_other, right_root, right_other, left_old, right_old, old_other)
+    )(left_root, right_root, left_old, right_old, packed)
+    other = [own_other] + [permute(mine[step], core_pairs()) for step in range(1, chips)]
     held = (mine, other)
     partial = call(
         kernel(start_update, first),
@@ -303,7 +303,7 @@
         (20 * order**3, 8 * order * order * 4),
         None,
         (ANY, ANY, VMEM, VMEM),
-    )(*mine, *other, left_kept, right_kept, other_kept)
+    )(*mine, *other, left_kept, right_kept, old_other)
     taken = permute(root_other, core_pairs())
     update, left_out, right_out = call(
         kernel(deliver, chips, order),
@@ -317,7 +317,7 @@
 
 
 def arrival(chips):
-    return list(range(chips // 2, chips)) + list(range(1, chips // 2))
+    return list(range(chips - 1, 0, -1))
 
 
 def solution(mesh):

time: 36.2 us -> 31.5 us (0.87)
  starting transfers between devices: 15.4 us -> 10.3 us
  waiting for transfers between devices: 10.7 us -> 11.3 us
    ppermute x14 -> x12, starting transfers between devices: 15.4 us -> 10.3 us  [permute(): return lax.ppermute(value, 'bcol', pairs)]
    convert_element_type x1, other arithmetic: 1.37 us -> 0.09 us  [step(): given_stat = jnp.where(half == 1, left_old, right_old).astype(BF16)]
    concatenate x0 -> x1, other arithmetic: none -> 1.16 us  [step(): packed = jnp.concatenate([pieces[0], left_root, right_root], 0)]
    ppermute x14 -> x12, waiting for transfers between devices: 10.7 us -> 11.3 us  [permute(): return lax.ppermute(value, 'bcol', pairs)]
  transfers between devices with their start and end apart: 14 -> 12, of which waited for: 7 -> 6; matrix products, arithmetic and copies ran while one was open for 4% -> 0% of each run, Pallas kernels for 4% -> 4%
where the time goes in v5:
time: 31.5 us; the launch traced here: 31.3 us
  waiting for transfers between devices  11.3 us (36%)
  starting transfers between devices  10.3 us (33%)
  Pallas kernels  6.15 us (20%)
  between operations  1.4 us (4%)
  other arithmetic  1.25 us (4%)
  local copies, waits for them, and re-layouts  0.96 us (3%)
    ppermute x12, waiting for transfers between devices, permute(): return lax.ppermute(value, 'bcol', pairs)  11.3 us
    ppermute x12, starting transfers between devices, permute(): return lax.ppermute(value, 'bcol', pairs)  10.3 us
    pallas_call x6, Pallas kernels, run(): pl.pallas_call(kernel, out_shape=out_shape, in_specs=ins or [VMEM] * len(...  6.15 us
    concatenate x1, other arithmetic, step(): packed = jnp.concatenate([pieces[0], left_root, right_root], 0)  1.16 us
    unnamed x10, local copies, waits for them, and re-layouts  0.96 us
  transfers between devices with their start and end apart: 12, of which 6 were waited for; matrix products, arithmetic and copies ran while one was open for 0% of the time, Pallas kernels for 4%

profile of v5, /device:TPU:0, one launch (start us, length us, event | category | flops | bytes accessed | tf_op | source)
XLA Modules:
  0.0 31.3 jit_solution(17966336116396213142)
XLA Ops:
  0.6 0.9 %copy-done.4 = bf16[64,2048]{1,0:T(8,128)(2,1)S(1)} copy-done((bf16[64,2048]{1,0:T(8,128)(2,1)S(1)}, bf16[64,2048]{1,0:T(8,128)(2,1)}, u32[]{:S(2)}) %copy-start.4) | copy-done | bytes 262168
  1.6 0.1 shard_map.101
  1.7 0.0 copy-start.2
  1.7 0.0 copy-start.3
  1.7 1.2 %pad_maximum_fusion = bf16[576,512]{1,0:T(8,128)(2,1)S(1)} fusion(bf16[256,512]{1,0:T(8,128)(2,1)} %bitcast.13, bf16[256,512]{1,0:T(8,128)(2,1)} %bitcast.10, bf16[64,512]{1,0:T(8,128)(2,1)S(1)} %get-tuple-element.26.refs_0_), kind=kLoop, calls=%fused_computation | loop fusion | flops 1769472 | bytes 1179648 | tf_op jit(solution)/shard_map/concatenate | solution.py:264
  2.9 0.6 %collective-permute-start.3 = (bf16[576,512]{1,0:T(8,128)(2,1)S(1)}, bf16[576,512]{1,0:T(8,128)(2,1)S(1)}, u32[]{:S(2)}, u32[]{:S(2)}) collective-permute-start(bf16[576,512]{1,0:T(8,128)(2,1)S(1)} %pad_maximum_fusion), channel_id=1, source_target_pairs={{0,1},{1,0},{2,3},{3,2},{4,5},{5,4},{6,7},{7,6},{8,9},{9,8},{10,11... | collective-permute-start | bytes 1769480 | tf_op jit(solution)/shard_map/ppermute | solution.py:32
  3.4 0.1 select_convert_fusion
  3.5 0.2 collective-permute-start.7
  3.7 5.0 %collective-permute-start.2 = (bf16[64,512]{1,0:T(8,128)(2,1)S(1)}, bf16[64,512]{1,0:T(8,128)(2,1)S(1)}, u32[]{:S(2)}, u32[]{:S(2)}) collective-permute-start(bf16[64,512]{1,0:T(8,128)(2,1)S(1)} %get-tuple-element.29), channel_id=1, source_target_pairs={{0,6},{1,7},{2,4},{3,5},{4,2},{5,3},{6,0},{7,1},{8,14},{9,15},{10,... | collective-permute-start | bytes 196616 | tf_op jit(solution)/shard_map/ppermute | solution.py:32
  8.7 0.6 %collective-permute-start.1 = (bf16[64,512]{1,0:T(8,128)(2,1)S(1)}, bf16[64,512]{1,0:T(8,128)(2,1)S(1)}, u32[]{:S(2)}, u32[]{:S(2)}) collective-permute-start(bf16[64,512]{1,0:T(8,128)(2,1)S(1)} %get-tuple-element.28), channel_id=1, source_target_pairs={{0,4},{1,5},{2,6},{3,7},{4,0},{5,1},{6,2},{7,3},{8,12},{9,13},{10,... | collective-permute-start | bytes 196616 | tf_op jit(solution)/shard_map/ppermute | solution.py:32
  9.3 2.4 %collective-permute-done.2.refs_3_ = bf16[64,512]{1,0:T(8,128)(2,1)S(1)} collective-permute-done((bf16[64,512]{1,0:T(8,128)(2,1)S(1)}, bf16[64,512]{1,0:T(8,128)(2,1)S(1)}, u32[]{:S(2)}, u32[]{:S(2)}) %collective-permute-start.2) | collective-permute-done | bytes 65568 | tf_op jit(solution)/shard_map/ppermute | solution.py:32
  11.6 2.0 %collective-permute-done.refs_1_ = bf16[64,512]{1,0:T(8,128)(2,1)S(1)} collective-permute-done((bf16[64,512]{1,0:T(8,128)(2,1)S(1)}, bf16[64,512]{1,0:T(8,128)(2,1)S(1)}, u32[]{:S(2)}, u32[]{:S(2)}) %collective-permute-start) | collective-permute-done | bytes 65568 | tf_op jit(solution)/shard_map/ppermute | solution.py:32
  13.6 0.0 collective-permute-start.4
  13.6 1.0 %collective-permute-done.1.refs_2_ = bf16[64,512]{1,0:T(8,128)(2,1)S(1)} collective-permute-done((bf16[64,512]{1,0:T(8,128)(2,1)S(1)}, bf16[64,512]{1,0:T(8,128)(2,1)S(1)}, u32[]{:S(2)}, u32[]{:S(2)}) %collective-permute-start.1) | collective-permute-done | bytes 65568 | tf_op jit(solution)/shard_map/ppermute | solution.py:32
  14.6 0.0 collective-permute-start.5
  14.6 0.0 collective-permute-done.3.refs_4_
  14.6 0.3 %shard_map.102 = (bf16[64,512]{1,0:T(8,128)(2,1)S(1)}, bf16[256,384]{1,0:T(8,128)(2,1)S(1)}, bf16[256,128]{1,0:T(8,128)(2,1)S(1)}, bf16[512,512]{1,0:T(8,128)(2,...) custom-call(bf16[256,512]{1,0:T(8,128)(2,1)S(1)} %bitcast.11, bf16[256,512]{1,0:T(8,128)(2,1)S(1)} %bitcast.14, ...), custom_call_target="tpu_custom_call" | custom-call | bytes 2097152 | tf_op jit(solution)/shard_map/pallas_call | solution.py:43
  14.9 0.0 collective-permute-done.6.refs_7_.refs_5_
  14.9 0.0 collective-permute-done.4.refs_5_.refs_1_
  14.9 0.9 %collective-permute-done.5.refs_6_.refs_0_ = bf16[64,512]{1,0:T(8,128)(2,1)S(1)} collective-permute-done((bf16[64,512]{1,0:T(8,128)(2,1)S(1)}, bf16[64,512]{1,0:T(8,128)(2,1)S(1)}, u32[]{:S(2)}, u32[]{:S(2)}) %collective-permute-start.5) | collective-permute-done | bytes 65568 | tf_op jit(solution)/shard_map/ppermute | solution.py:32
  15.8 0.0 collective-permute-done.7.refs_10_
  15.8 3.8 %shard_map.103 = (f32[256,512]{1,0:T(8,128)}, f32[256,512]{1,0:T(8,128)}, bf16[256,512]{1,0:T(8,128)(2,1)S(1)}, bf16[256,512]{1,0:T(8,128)(2,1)S(1)}) custom-call(bf16[64,512]{1,0:T(8,128)(2,1)S(1)} %get-tuple-element.26.refs_0_, bf16[64,512]{1,0:T(8,128)(2,1)S(1)} %collective-permute-done.refs_1_, bf16[64,512]{1,0:T(8,128)(2,1)S(1)} %collective-permute-done.1.refs_2_, ...), custom_call_target="tpu_custom_call" | custom-call | flops 2684354560 | bytes 8388608 | tf_op jit(solution)/shard_map/pallas_call | solution.py:43
  19.6 0.2 collective-permute-start.8
  19.8 0.6 %shard_map.104.refs_4_ = f32[256,512]{1,0:T(8,128)S(1)} custom-call(bf16[64,512]{1,0:T(8,128)(2,1)S(1)} %get-tuple-element.26.refs_0_, bf16[64,512]{1,0:T(8,128)(2,1)S(1)} %collective-permute-done.refs_1_, bf16[64,512]{1,0:T(8,128)(2,1)S(1)} %collective-permute-done.1.refs_2_, bf16[64,512]{1,0:T(8,128)(2,1)S(1)} %collective-permute-done.2.refs_3_, ...), custom_call_target="tpu_custom_call" | custom-call | flops 301989888 | bytes 2097152 | tf_op jit(solution)/shard_map/pallas_call | solution.py:43
  20.4 0.4 %shard_map.105 = (bf16[64,512]{1,0:T(8,128)(2,1)S(1)}, bf16[64,512]{1,0:T(8,128)(2,1)S(1)}, bf16[64,512]{1,0:T(8,128)(2,1)S(1)}, bf16[64,512]{1,0:T(8,128)(2,1)S(1)}) custom-call(bf16[64,512]{1,0:T(8,128)(2,1)S(1)} %collective-permute-done.5.refs_6_.refs_0_, bf16[64,512]{1,0:T(8,128)(2,1)S(1)} %collective-permute-done.4.refs_5_.refs_1_, ...), custom_call_target="tpu_custom_call" | custom-call | flops 100663296 | bytes 2097152 | tf_op jit(solution)/shard_map/pallas_call | solution.py:43
  20.9 2.0 %collective-permute-start.10 = (bf16[64,512]{1,0:T(8,128)(2,1)S(1)}, bf16[64,512]{1,0:T(8,128)(2,1)S(1)}, u32[]{:S(2)}, u32[]{:S(2)}) collective-permute-start(bf16[64,512]{1,0:T(8,128)(2,1)S(1)} %get-tuple-element.40), channel_id=1, source_target_pairs={{0,4},{1,5},{2,6},{3,7},{4,0},{5,1},{6,2},{7,3},{8,12},{9,13},{10,... | collective-permute-start | bytes 196616 | tf_op jit(solution)/shard_map/ppermute | solution.py:32
  22.9 1.8 %collective-permute-start.11 = (bf16[64,512]{1,0:T(8,128)(2,1)S(1)}, bf16[64,512]{1,0:T(8,128)(2,1)S(1)}, u32[]{:S(2)}, u32[]{:S(2)}) collective-permute-start(bf16[64,512]{1,0:T(8,128)(2,1)S(1)} %get-tuple-element.41), channel_id=1, source_target_pairs={{0,6},{1,7},{2,4},{3,5},{4,2},{5,3},{6,0},{7,1},{8,14},{9,15},{10,... | collective-permute-start | bytes 196616 | tf_op jit(solution)/shard_map/ppermute | solution.py:32
  24.6 0.0 collective-permute-start.9
  25.3 4.2 %collective-permute-done.10.refs_7_ = bf16[64,512]{1,0:T(8,128)(2,1)S(1)} collective-permute-done((bf16[64,512]{1,0:T(8,128)(2,1)S(1)}, bf16[64,512]{1,0:T(8,128)(2,1)S(1)}, u32[]{:S(2)}, u32[]{:S(2)}) %collective-permute-start.10) | collective-permute-done | bytes 65568 | tf_op jit(solution)/shard_map/ppermute | solution.py:32
  29.5 0.8 %collective-permute-done.9.refs_6_ = bf16[64,512]{1,0:T(8,128)(2,1)S(1)} collective-permute-done((bf16[64,512]{1,0:T(8,128)(2,1)S(1)}, bf16[64,512]{1,0:T(8,128)(2,1)S(1)}, u32[]{:S(2)}, u32[]{:S(2)}) %collective-permute-start.9) | collective-permute-done | bytes 65568 | tf_op jit(solution)/shard_map/ppermute | solution.py:32
  30.4 0.0 collective-permute-done.8.refs_4_
  30.4 0.9 %shard_map.106 = (bf16[64,2048]{1,0:T(8,128)(2,1)}, bf16[256,512]{1,0:T(8,128)(2,1)}, bf16[256,512]{1,0:T(8,128)(2,1)}) custom-call(s32[1,1]{1,0:T(1,128)S(6)} %copy.11.refs_0_, bf16[256,512]{1,0:T(8,128)(2,1)S(1)} %bitcast.12, bf16[256,512]{1,0:T(8,128)(2,1)S(1)} %bitcast.15, bf16[256,512]{1,0:T(8,128)(2,1)S(1)} %get-tuple-element.33.refs_3_, ...), custom_call_target="tpu_custom_call" | custom-call | bytes 2097152 | tf_op jit(solution)/shard_map/pallas_call | solution.py:43
  (10 shorter events, 0.0 us)
Async XLA Ops:
  0.6 1.0 %copy-start.4 = (bf16[64,2048]{1,0:T(8,128)(2,1)S(1)}, bf16[64,2048]{1,0:T(8,128)(2,1)}, u32[]{:S(2)}) copy-start(bf16[64,2048]{1,0:T(8,128)(2,1)} %refs_0_.2) | copy-start | bytes 786436
  1.7 1.7 %copy-start.2 = (f32[1,256,512]{2,1,0:T(8,128)S(1)}, f32[1,256,512]{2,1,0:T(8,128)}, u32[]{:S(2)}) copy-start(f32[1,256,512]{2,1,0:T(8,128)} %param.7) | copy-start | bytes 1572868
  1.7 1.7 %copy-start.3 = (f32[1,256,512]{2,1,0:T(8,128)S(1)}, f32[1,256,512]{2,1,0:T(8,128)}, u32[]{:S(2)}) copy-start(f32[1,256,512]{2,1,0:T(8,128)} %param.8) | copy-start | bytes 1572868
  2.9 11.7 %collective-permute-start.3 = (bf16[576,512]{1,0:T(8,128)(2,1)S(1)}, bf16[576,512]{1,0:T(8,128)(2,1)S(1)}, u32[]{:S(2)}, u32[]{:S(2)}) collective-permute-start(bf16[576,512]{1,0:T(8,128)(2,1)S(1)} %pad_maximum_fusion), channel_id=1, source_target_pairs={{0,1},{1,0},{2,3},{3,2},{4,5},{5,4},{6,7},{7,6},{8,9},{9,8},{10,11... | collective-permute-start | bytes 1769480 | tf_op jit(solution)/shard_map/ppermute | solution.py:32
  3.4 11.1 %copy-start = (bf16[1,256,512]{2,1,0:T(8,128)(2,1)S(1)}, bf16[1,256,512]{2,1,0:T(8,128)(2,1)}, u32[]{:S(2)}) copy-start(bf16[1,256,512]{2,1,0:T(8,128)(2,1)} %param.9) | copy-start | bytes 786436
  3.4 11.2 %copy-start.1 = (bf16[1,256,512]{2,1,0:T(8,128)(2,1)S(1)}, bf16[1,256,512]{2,1,0:T(8,128)(2,1)}, u32[]{:S(2)}) copy-start(bf16[1,256,512]{2,1,0:T(8,128)(2,1)} %param.10) | copy-start | bytes 786436
  3.5 12.3 %collective-permute-start.7 = (bf16[256,512]{1,0:T(8,128)(2,1)S(1)}, bf16[256,512]{1,0:T(8,128)(2,1)S(1)}, u32[]{:S(2)}, u32[]{:S(2)}) collective-permute-start(bf16[256,512]{1,0:T(8,128)(2,1)S(1)} %select_convert_fusion), channel_id=1, source_target_pairs={{0,1},{1,0},{2,3},{3,2},{4,5},{5,4},{6,7},{7,6},{8,9},{9,8},{10,11... | collective-permute-start | bytes 786440 | tf_op jit(solution)/shard_map/ppermute | solution.py:32
  3.7 7.9 %collective-permute-start.2 = (bf16[64,512]{1,0:T(8,128)(2,1)S(1)}, bf16[64,512]{1,0:T(8,128)(2,1)S(1)}, u32[]{:S(2)}, u32[]{:S(2)}) collective-permute-start(bf16[64,512]{1,0:T(8,128)(2,1)S(1)} %get-tuple-element.29), channel_id=1, source_target_pairs={{0,6},{1,7},{2,4},{3,5},{4,2},{5,3},{6,0},{7,1},{8,14},{9,15},{10,... | collective-permute-start | bytes 196616 | tf_op jit(solution)/shard_map/ppermute | solution.py:32
  8.7 4.9 %collective-permute-start = (bf16[64,512]{1,0:T(8,128)(2,1)S(1)}, bf16[64,512]{1,0:T(8,128)(2,1)S(1)}, u32[]{:S(2)}, u32[]{:S(2)}) collective-permute-start(bf16[64,512]{1,0:T(8,128)(2,1)S(1)} %get-tuple-element.27), channel_id=1, source_target_pairs={{0,2},{1,3},{2,0},{3,1},{4,6},{5,7},{6,4},{7,5},{8,10},{9,11},{10,... | collective-permute-start | bytes 196616 | tf_op jit(solution)/shard_map/ppermute | solution.py:32
  8.7 5.9 %collective-permute-start.1 = (bf16[64,512]{1,0:T(8,128)(2,1)S(1)}, bf16[64,512]{1,0:T(8,128)(2,1)S(1)}, u32[]{:S(2)}, u32[]{:S(2)}) collective-permute-start(bf16[64,512]{1,0:T(8,128)(2,1)S(1)} %get-tuple-element.28), channel_id=1, source_target_pairs={{0,4},{1,5},{2,6},{3,7},{4,0},{5,1},{6,2},{7,3},{8,12},{9,13},{10,... | collective-permute-start | bytes 196616 | tf_op jit(solution)/shard_map/ppermute | solution.py:32
  11.6 3.3 %collective-permute-start.6 = (bf16[64,512]{1,0:T(8,128)(2,1)S(1)}, bf16[64,512]{1,0:T(8,128)(2,1)S(1)}, u32[]{:S(2)}, u32[]{:S(2)}) collective-permute-start(bf16[64,512]{1,0:T(8,128)(2,1)S(1)} %collective-permute-done.2.refs_3_), channel_id=1, source_target_pairs={{0,1},{1,0},{2,3},{3,2},{4,5},{5,4},{6,7},{7,6},{8,9},{9,8},{10,11... | collective-permute-start | bytes 196616 | tf_op jit(solution)/shard_map/ppermute | solution.py:32
  13.6 1.3 %collective-permute-start.4 = (bf16[64,512]{1,0:T(8,128)(2,1)S(1)}, bf16[64,512]{1,0:T(8,128)(2,1)S(1)}, u32[]{:S(2)}, u32[]{:S(2)}) collective-permute-start(bf16[64,512]{1,0:T(8,128)(2,1)S(1)} %collective-permute-done.refs_1_), channel_id=1, source_target_pairs={{0,1},{1,0},{2,3},{3,2},{4,5},{5,4},{6,7},{7,6},{8,9},{9,8},{10,11... | collective-permute-start | bytes 196616 | tf_op jit(solution)/shard_map/ppermute | solution.py:32
  14.6 1.3 %collective-permute-start.5 = (bf16[64,512]{1,0:T(8,128)(2,1)S(1)}, bf16[64,512]{1,0:T(8,128)(2,1)S(1)}, u32[]{:S(2)}, u32[]{:S(2)}) collective-permute-start(bf16[64,512]{1,0:T(8,128)(2,1)S(1)} %collective-permute-done.1.refs_2_), channel_id=1, source_target_pairs={{0,1},{1,0},{2,3},{3,2},{4,5},{5,4},{6,7},{7,6},{8,9},{9,8},{10,11... | collective-permute-start | bytes 196616 | tf_op jit(solution)/shard_map/ppermute | solution.py:32
  19.6 10.8 %collective-permute-start.8 = (bf16[256,512]{1,0:T(8,128)(2,1)S(1)}, bf16[256,512]{1,0:T(8,128)(2,1)S(1)}, u32[]{:S(2)}, u32[]{:S(2)}) collective-permute-start(bf16[256,512]{1,0:T(8,128)(2,1)S(1)} %get-tuple-element.34), channel_id=1, source_target_pairs={{0,1},{1,0},{2,3},{3,2},{4,5},{5,4},{6,7},{7,6},{8,9},{9,8},{10,11... | collective-permute-start | bytes 786440 | tf_op jit(solution)/shard_map/ppermute | solution.py:32
  20.9 8.7 %collective-permute-start.10 = (bf16[64,512]{1,0:T(8,128)(2,1)S(1)}, bf16[64,512]{1,0:T(8,128)(2,1)S(1)}, u32[]{:S(2)}, u32[]{:S(2)}) collective-permute-start(bf16[64,512]{1,0:T(8,128)(2,1)S(1)} %get-tuple-element.40), channel_id=1, source_target_pairs={{0,4},{1,5},{2,6},{3,7},{4,0},{5,1},{6,2},{7,3},{8,12},{9,13},{10,... | collective-permute-start | bytes 196616 | tf_op jit(solution)/shard_map/ppermute | solution.py:32
  22.9 6.7 %collective-permute-start.11 = (bf16[64,512]{1,0:T(8,128)(2,1)S(1)}, bf16[64,512]{1,0:T(8,128)(2,1)S(1)}, u32[]{:S(2)}, u32[]{:S(2)}) collective-permute-start(bf16[64,512]{1,0:T(8,128)(2,1)S(1)} %get-tuple-element.41), channel_id=1, source_target_pairs={{0,6},{1,7},{2,4},{3,5},{4,2},{5,3},{6,0},{7,1},{8,14},{9,15},{10,... | collective-permute-start | bytes 196616 | tf_op jit(solution)/shard_map/ppermute | solution.py:32
  24.6 5.7 %collective-permute-start.9 = (bf16[64,512]{1,0:T(8,128)(2,1)S(1)}, bf16[64,512]{1,0:T(8,128)(2,1)S(1)}, u32[]{:S(2)}, u32[]{:S(2)}) collective-permute-start(bf16[64,512]{1,0:T(8,128)(2,1)S(1)} %get-tuple-element.39), channel_id=1, source_target_pairs={{0,2},{1,3},{2,0},{3,1},{4,6},{5,7},{6,4},{7,5},{8,10},{9,11},{10,... | collective-permute-start | bytes 196616 | tf_op jit(solution)/shard_map/ppermute | solution.py:32
